TPU v7x, 256 devices: a whole 4x4x8 slice. The times are simulated.
256 devices in a mesh: stn: 8 (over z), tm: 32 (over y, x, core).
Axes of the slice: x: 4, y: 4, z: 8, core: 2. Of those that a mesh axis runs over, the one named last changes fastest.
Arguments:
- voltages: bfloat16 [512, 2, 2, 256, 2048], P('tm', None, None, 'stn'), may hold values from -6 to 6
- taps: float32 [16, 2048], replicated, may hold values from -1.5 to 1.5
- sk_tolerance: float32 [384], P('tm'), may hold values from 0.05 to 0.3
- station_coords: int32 [256, 2], replicated, may hold values from 0 to 1023
- pointings: int32 [256, 2], replicated, may hold values from -64 to 64
- station_flags: int32 [256], replicated, may hold values 0 or 1
Outputs:
- beam_power: float32 [384, 32, 256], P('tm', None, 'stn')
All inputs are finite; a program needn't handle non-finite values.
Results may differ from a plain program's by a relative error of at most 0.0045.
Values may be sent and summed in bfloat16 or wider, within the bound.
No kernel may reach another device: no remote copies, remote signals or barrier semaphores. Data moves between devices by JAX's collectives and lax.ppermute only.
A program may use at most 128 MiB of HBM per device.

v0:
```python
import functools
import math

import jax
import jax.numpy as jnp
import numpy as np
from jax import lax
from jax.experimental import pallas as pl
from jax.experimental.pallas import tpu as pltpu
from jax.sharding import PartitionSpec as P

STATIONS = 256
NFFT = 2048
CHAN = 384
BEAMS = 256
INTEG = 16
TAPS = 16
FRAMES = 16
N_STN = 8
N_TM = 32
S_DEV = 32
LOCAL_CHAN = CHAN // N_STN
OWNED = CHAN // N_TM
WINDOW = 16
RADIX = 4
POINTS = NFFT // RADIX
SEGS = 4
F32 = jnp.float32
BF16 = jnp.bfloat16

EVEN = (0, 4, 1, 5, 10, 11)
ODD = (2, 6, 3, 7, 8, 9)


def stn_of(offset, t):
    if offset in EVEN:
        return 2 * ((EVEN.index(offset) + t) % 4)
    return 2 * ((ODD.index(offset) + t) % 4) + 1


def slot_of(offset):
    return 1 if offset >= 8 else 0


def channel_plan():
    channels, slots, sizes = [], [], []
    for k in range(N_STN):
        mine, places, count = [], [], []
        for residue in range(RADIX):
            before = len(mine)
            for t in range(N_TM):
                for offset in range(residue, OWNED, RADIX):
                    if stn_of(offset, t) == k:
                        mine.append(OWNED * t + offset)
                        places.append(N_TM * slot_of(offset) + t)
            count.append(len(mine) - before)
        assert len(mine) == LOCAL_CHAN and len(set(places)) == LOCAL_CHAN
        assert all(n % 8 == 0 for n in count)
        channels.append(mine)
        slots.append(places)
        sizes.append(count)
    return channels, slots, sizes


CHANNELS, SLOTS, SIZES = channel_plan()
ORDER = [sorted(range(LOCAL_CHAN), key=lambda n, mine=mine: mine[n]) for mine in CHANNELS]
VISITED = [[mine[n] for n in order] for mine, order in zip(CHANNELS, ORDER)]
VISITED_SLOTS = [[places[n] for n in order] for places, order in zip(SLOTS, ORDER)]


def dft_tables():
    tables = []
    points = np.arange(POINTS)
    for residue in range(RADIX):
        order = []
        for k in range(N_STN):
            start = sum(SIZES[k][:residue])
            order += CHANNELS[k][start : start + SIZES[k][residue]]
        turns = (np.array(order)[:, None] * points[None, :]) % NFFT
        angle = 2.0 * np.pi * turns / NFFT
        cosine = np.cos(angle) / math.sqrt(NFFT)
        sine = np.sin(angle) / math.sqrt(NFFT)
        real_rows = np.stack([cosine, sine], 1)
        imag_rows = np.stack([-sine, cosine], 1)
        columns = np.zeros((2 * POINTS, 256))
        for part, rows in enumerate((real_rows, imag_rows)):
            rows = rows.reshape(-1, 2, POINTS // 128, 128).transpose(2, 1, 3, 0)
            columns[:, 128 * part : 128 * part + CHAN // RADIX] = rows.reshape(2 * POINTS, -1)
        tables.append(columns)
    return np.stack(tables, 0).astype(np.float32).astype(jnp.bfloat16)


def lane_permutation():
    source = np.arange(N_STN * 128)
    d, f4, s = source // 128, source // 32 % 4, source % 32
    target = f4 * STATIONS + d * S_DEV + s
    onehot = np.zeros((N_STN * 128, 4 * STATIONS), np.float32)
    onehot[source, target] = 1.0
    return onehot.astype(jnp.bfloat16)


def packed_sums(first, second):
    lane = lax.broadcasted_iota(jnp.int32, (LOCAL_CHAN, 128), 1)
    packed = None
    for group, total in enumerate((first[0], first[1], second[0], second[1])):
        total = total + pltpu.roll(total, 64, 1)
        total = total + pltpu.roll(total, 32, 1)
        packed = total if group == 0 else jnp.where(lane // 32 == group, total, packed)
    return packed


def channelize_kernel(carried, polar, *refs):
    if not carried:
        me_ref, refs = refs[0], refs[1:]
    v_refs, tap_refs, table_ref = refs[:RADIX], refs[RADIX : 2 * RADIX], refs[2 * RADIX]
    mixed, filtered, tables, arrival = refs[-4:]
    extra = refs[2 * RADIX + 1 : -4]
    if carried:
        (out_ref,) = extra
    elif polar == 0:
        received_ref, out_ref, sums_ref = extra
    else:
        received_ref, before_ref, tol_ref, out_ref, packed_ref, sums_ref = extra
    step = pl.program_id(0)
    outputs = FRAMES - 1 if carried else FRAMES
    load = pltpu.make_async_copy(table_ref, tables, arrival)

    @pl.when(step == 0)
    def _():
        load.start()

    def rows_chunk(chunk, _):
        row = pl.multiple_of(chunk * 16, 16)
        for j in range(RADIX):
            taps = [jnp.broadcast_to(tap_refs[j][k : k + 1, :], (16, 128)) for k in range(TAPS)]
            for r in range(2):
                x = [v_refs[j][f, r, 0, pl.ds(row, 16), :].astype(F32) for f in range(FRAMES)]
                for g in range(outputs):
                    if carried:
                        pairs = [(k, FRAMES + g - k) for k in range(g + 1, TAPS)]
                    else:
                        pairs = [(k, g - k) for k in range(g + 1)]
                    total = taps[pairs[0][0]] * x[pairs[0][1]]
                    for k, f in pairs[1:]:
                        total = total + taps[k] * x[f]
                    filtered[r, j, g] = total
        column = pl.multiple_of(step * 256, 256)
        for g in range(outputs):
            re = [filtered[0, j, g] for j in range(RADIX)]
            im = [filtered[1, j, g] for j in range(RADIX)]
            ar, ai = re[0] + re[2], im[0] + im[2]
            br, bi = re[0] - re[2], im[0] - im[2]
            cr, ci = re[1] + re[3], im[1] + im[3]
            dr, di = re[1] - re[3], im[1] - im[3]
            parts = (
                (ar + cr, ai + ci),
                (br + di, bi - dr),
                (ar - cr, ai - ci),
                (br - di, bi + dr),
            )
            target = pl.multiple_of(g * S_DEV + row, 16)
            for residue, (y_re, y_im) in enumerate(parts):
                mixed[residue, pl.ds(target, 16), pl.ds(column, 128)] = y_re.astype(BF16)
                mixed[residue, pl.ds(target, 16), pl.ds(column + 128, 128)] = y_im.astype(BF16)
        return 0

    lax.fori_loop(0, S_DEV // 16, rows_chunk, 0)

    @pl.when(step == pl.num_programs(0) - 1)
    def _():
        load.wait()
        if carried:
            for residue in range(RADIX):
                mixed[residue, outputs * S_DEV :, :] = jnp.zeros((S_DEV, 2 * POINTS), BF16)
        else:
            sums_ref[...] = jnp.zeros_like(sums_ref)
        for residue in range(RADIX):
            product = jnp.dot(mixed[residue], tables[residue], preferred_element_type=F32)
            for seg in range(SEGS):
                rows = product[seg * 128 : seg * 128 + 128]
                turned = (rows[:, :128].T, rows[:, 128:].T)
                row = 0
                for k in range(N_STN):
                    size = SIZES[k][residue]
                    start = sum(SIZES[k][:residue])
                    power = None
                    for part in range(2):
                        at = part * LOCAL_CHAN + start
                        piece = turned[part][row : row + size]
                        if not carried:
                            piece = piece + received_ref[k, seg, at : at + size, :].astype(F32)
                        piece = piece.astype(BF16)
                        out_ref[k, seg, at : at + size, :] = piece
                        if not carried:
                            value = piece.astype(F32)
                            power = value * value if power is None else power + value * value
                    if not carried:
                        place = lax.rem(k + N_STN - me_ref[0], N_STN)
                        sums_ref[place, 0, start : start + size, :] += power
                        sums_ref[place, 1, start : start + size, :] += power * power
                    row += size
        if not carried and polar == 1:
            for d in range(N_STN):
                packed_ref[d] = packed_sums(before_ref[d], sums_ref[d])
            packed_ref[N_STN] = tol_ref[...]


def channelize(voltages, taps, table, polar, received=None, me=None, before=None, tolerances=None):
    carried = received is None
    steps = POINTS // 128
    v_specs = [
        pl.BlockSpec((FRAMES, 2, 1, S_DEV, 128), functools.partial(lambda j, i: (0, 0, polar, 0, j * steps + i), j))
        for j in range(RADIX)
    ]
    t_specs = [
        pl.BlockSpec((TAPS, 128), functools.partial(lambda j, i: (0, j * steps + i), j)) for j in range(RADIX)
    ]
    whole = pl.BlockSpec(memory_space=pl.ANY)
    table = pltpu.with_memory_space_constraint(table, pltpu.HBM)
    vmem = pl.BlockSpec(memory_space=pltpu.VMEM)
    shape = jax.ShapeDtypeStruct((N_STN, SEGS, 2 * LOCAL_CHAN, 128), BF16)
    in_specs = v_specs + t_specs + [whole]
    voltages = pltpu.with_memory_space_constraint(voltages, pltpu.HBM)
    operands = [voltages] * RADIX + [taps] * RADIX + [table]
    outs, out_specs, scratch = [shape], [vmem], []
    if not carried:
        in_specs = [pl.BlockSpec(memory_space=pltpu.SMEM)] + in_specs + [vmem]
        operands = [me] + operands + [received]
        out_specs.append(vmem)
        if polar == 0:
            outs.append(jax.ShapeDtypeStruct((N_STN, 2, LOCAL_CHAN, 128), F32))
        else:
            in_specs += [vmem, vmem]
            operands += [before, tolerances]
            outs.append(jax.ShapeDtypeStruct((N_STN + 1, LOCAL_CHAN, 128), F32))
            scratch.append(pltpu.VMEM((N_STN, 2, LOCAL_CHAN, 128), F32))
    return pl.pallas_call(
        functools.partial(channelize_kernel, carried, polar),
        out_shape=outs,
        grid=(steps,),
        in_specs=in_specs,
        out_specs=out_specs,
        scratch_shapes=scratch
        + [
            pltpu.VMEM((RADIX, FRAMES * S_DEV, 2 * POINTS), BF16),
            pltpu.VMEM((2, RADIX, FRAMES, 16, 128), F32),
            pltpu.VMEM(table.shape, BF16),
            pltpu.SemaphoreType.DMA(()),
        ],
        compiler_params=pltpu.CompilerParams(
            dimension_semantics=("arbitrary",), vmem_limit_bytes=36 * 1024 * 1024
        ),
        cost_estimate=pl.CostEstimate(flops=12_000_000_000, bytes_accessed=8_000_000, transcendentals=0),
        name="carried" if carried else "own",
    )(*operands)


STATION_ROWS = 32


def turn(offsets, number):
    unit = 2.0 * math.pi / 65536.0
    residue = (offsets * number) & 65535
    quadrant = (residue + 8192) >> 14
    angle = (residue - (quadrant << 14)).astype(F32) * unit
    square = angle * angle
    sine = angle * (1.0 + square * (-1.0 / 6.0 + square * (1.0 / 120.0 - square * (1.0 / 5040.0))))
    cosine = 1.0 + square * (
        -0.5 + square * (1.0 / 24.0 + square * (-1.0 / 720.0 + square * (1.0 / 40320.0)))
    )
    odd = (quadrant & 1) == 1
    real = jnp.where(odd, sine, cosine)
    imag = jnp.where(odd, cosine, sine)
    real = jnp.where(((quadrant + 1) & 2) == 2, -real, real)
    imag = jnp.where((quadrant & 2) == 2, -imag, imag)
    return real, imag


def times(a, b):
    return a[0] * b[0] - a[1] * b[1], a[0] * b[1] + a[1] * b[0]


def steering_kernel(t_ref, o_ref, offset_ref, gain_ref, out_ref, coarse, fine):
    offsets = offset_ref[...]
    single = turn(offsets, 1)
    stride = turn(offsets, OWNED)
    fast = turn(offsets, 4 * OWNED)
    gain = gain_ref[...]
    value = (gain, jnp.zeros_like(gain))
    for t in range(4):
        coarse[t, 0], coarse[t, 1] = value
        if t < 3:
            value = times(value, stride)

    def advance(n, _):
        for i in range(4):
            t = 4 * n + i
            coarse[t, 0], coarse[t, 1] = times((coarse[t - 4, 0], coarse[t - 4, 1]), fast)
        return 0

    lax.fori_loop(1, N_TM // 4, advance, 0)
    pair = times(single, single)
    fine[0, 0], fine[0, 1] = single
    fine[1, 0], fine[1, 1] = pair
    for o in range(2, OWNED):
        fine[o, 0], fine[o, 1] = times((fine[o - 2, 0], fine[o - 2, 1]), pair)

    def channels(n, _):
        for i in range(4):
            at = 4 * n + i
            t, o = t_ref[at], o_ref[at]
            real, imag = times((coarse[t, 0], coarse[t, 1]), (fine[o, 0], fine[o, 1]))
            out_ref[at, :, :BEAMS] = real.astype(BF16)
            out_ref[at, :, BEAMS:] = imag.astype(BF16)
        return 0

    lax.fori_loop(0, LOCAL_CHAN // 4, channels, 0)


def steering(owners, places, offsets, gain):
    smem = pl.BlockSpec(memory_space=pltpu.SMEM)
    rows = pl.BlockSpec((STATION_ROWS, BEAMS), lambda i: (i, 0))
    return pl.pallas_call(
        steering_kernel,
        out_shape=jax.ShapeDtypeStruct((LOCAL_CHAN, STATIONS, 2 * BEAMS), BF16),
        grid=(STATIONS // STATION_ROWS,),
        in_specs=[smem, smem, rows, rows],
        out_specs=pl.BlockSpec((LOCAL_CHAN, STATION_ROWS, 2 * BEAMS), lambda i: (0, i, 0)),
        scratch_shapes=[
            pltpu.VMEM((N_TM, 2, STATION_ROWS, BEAMS), F32),
            pltpu.VMEM((OWNED, 2, STATION_ROWS, BEAMS), F32),
        ],
        compiler_params=pltpu.CompilerParams(
            dimension_semantics=("arbitrary",), vmem_limit_bytes=54 * 1024 * 1024
        ),
        cost_estimate=pl.CostEstimate(flops=40_000, bytes_accessed=12_600, transcendentals=0),
        name="steering",
    )(owners, places, offsets, gain)


def place_stations(in_ref, perm_ref, out_ref):
    for seg in range(SEGS):
        stacked = jnp.concatenate([in_ref[g, seg] for g in range(N_STN)], 1)
        moved = jnp.dot(stacked, perm_ref[...], preferred_element_type=F32)
        for part in range(2):
            rows = moved[part * LOCAL_CHAN : (part + 1) * LOCAL_CHAN]
            for f4 in range(4):
                at = ((part * 4 + f4) * SEGS + seg) * LOCAL_CHAN
                for half in range(2):
                    column = f4 * STATIONS + half * 128
                    out_ref[half, at : at + LOCAL_CHAN, :] = rows[:, column : column + 128]


PLACED = (2, 32 * LOCAL_CHAN, 128)


def gather(blocks, perm):
    vmem = pl.BlockSpec(memory_space=pltpu.VMEM)
    return pl.pallas_call(
        place_stations,
        out_shape=jax.ShapeDtypeStruct(PLACED, F32),
        in_specs=[vmem] * 2,
        out_specs=vmem,
        compiler_params=pltpu.CompilerParams(vmem_limit_bytes=8 * 1024 * 1024),
        cost_estimate=pl.CostEstimate(flops=800_000_000, bytes_accessed=4_000_000, transcendentals=0),
        name="stations",
    )(blocks, perm)


BLOCK = 8
CHUNKS = LOCAL_CHAN // BLOCK


def beam_kernel(me_ref, chan_ref, slot_ref, order_ref, tol_ref, *refs):
    sum_refs = refs[:N_STN]
    first_ref, second_ref, perm_ref, weight_ref, out_ref = refs[N_STN : N_STN + 5]
    window_sums, ordered, second_placed, weights, powers, arrival = refs[N_STN + 5 :]

    def load(chunk):
        part = pl.ds(chunk * BLOCK, BLOCK)
        return pltpu.make_async_copy(weight_ref.at[part], weights.at[part], arrival.at[chunk])

    for chunk in range(CHUNKS):
        load(chunk).start()
    place_stations(second_ref, perm_ref, second_placed)
    powers[...] = jnp.zeros_like(powers)
    lane = lax.broadcasted_iota(jnp.int32, (LOCAL_CHAN, 128), 1)
    for d in range(N_STN):
        ordered[lax.rem(me_ref[0] + N_STN - d, N_STN)] = sum_refs[d][...]
    for polar in range(2):
        for kind in range(2):
            group = 2 * polar + kind
            for half in range(2):
                total = jnp.zeros((LOCAL_CHAN, 128), F32)
                for place in range(4):
                    shift = 32 * ((place - group) % 4)
                    piece = ordered[4 * half + place]
                    if shift:
                        piece = pltpu.roll(piece, shift, 1)
                    total = jnp.where(lane // 32 == place, piece, total)
                window_sums[polar, kind, :, half * 128 : half * 128 + 128] = total

    size = float(WINDOW * FRAMES)

    def visit_chunk(chunk, _):
        load(chunk).wait()
        for inner in range(BLOCK):
            visit = chunk * BLOCK + inner
            local = order_ref[visit]
            tolerance = tol_ref[chan_ref[visit]]
            rows = []
            for polar, ref in enumerate((first_ref, second_placed)):
                s1 = window_sums[polar, 0, pl.ds(local, 1), :]
                s2 = window_sums[polar, 1, pl.ds(local, 1), :]
                kurtosis = (size + 1.0) / (size - 1.0) * (size * s2 / (s1 * s1) - 1.0)
                deviation = (kurtosis - 1.0) / tolerance
                soft = 1.0 / (1.0 + deviation * deviation)
                halves = [ref[half, pl.ds(local, 32, stride=LOCAL_CHAN), :] for half in range(2)]
                values = jnp.concatenate(halves, 1)
                rows.append((values * soft).astype(BF16))
            stacked = jnp.concatenate([rows[0][:16], rows[1][:16], rows[0][16:], rows[1][16:]], 0)
            product = jnp.dot(stacked, weights[visit], preferred_element_type=F32)
            real = product[:32, :BEAMS] - product[32:, BEAMS:]
            imag = product[:32, BEAMS:] + product[32:, :BEAMS]
            power = jnp.sum(real * real + imag * imag, 0, keepdims=True) * (1.0 / (2.0 * INTEG))
            powers[pl.ds(slot_ref[visit], 1), :] = power
        return 0

    lax.fori_loop(0, CHUNKS, visit_chunk, 0)
    share = BEAMS // N_STN
    out_ref[...] = jnp.zeros_like(out_ref)
    for slot in range(2):
        rows = powers[slot * N_TM : (slot + 1) * N_TM, :]
        for j in range(N_STN):
            out_ref[:, j, slot * share : (slot + 1) * share] = rows[:, j * share : (j + 1) * share]


def beams(me, channels, slots, order, tolerance, sums, first, second, perm, weights):
    smem = pl.BlockSpec(memory_space=pltpu.SMEM)
    vmem = pl.BlockSpec(memory_space=pltpu.VMEM)
    weights = pltpu.with_memory_space_constraint(weights, pltpu.HBM)
    return pl.pallas_call(
        beam_kernel,
        out_shape=jax.ShapeDtypeStruct((N_TM, N_STN, 128), F32),
        in_specs=[smem] * 5 + [vmem] * (N_STN + 3) + [pl.BlockSpec(memory_space=pl.ANY)],
        out_specs=vmem,
        scratch_shapes=[
            pltpu.VMEM((2, 2, LOCAL_CHAN, STATIONS), F32),
            pltpu.VMEM((N_STN, LOCAL_CHAN, 128), F32),
            pltpu.VMEM(PLACED, F32),
            pltpu.VMEM((LOCAL_CHAN, STATIONS, 2 * BEAMS), BF16),
            pltpu.VMEM((2 * N_TM, BEAMS), F32),
            pltpu.SemaphoreType.DMA((CHUNKS,)),
        ],
        compiler_params=pltpu.CompilerParams(vmem_limit_bytes=36 * 1024 * 1024),
        cost_estimate=pl.CostEstimate(flops=2_400_000_000, bytes_accessed=16_000_000, transcendentals=0),
        name="beams",
    )(me, channels, slots, order, tolerance, *sums, first, second, perm, weights)


def settle_kernel(t_ref, in_ref, out_ref):
    for offset in range(OWNED):
        group = EVEN if offset in EVEN else ODD
        parity = 0 if offset in EVEN else 1
        k = 2 * lax.rem(group.index(offset) + t_ref[0], 4) + parity
        column = slot_of(offset) * 32
        out_ref[offset] = in_ref[pl.ds(k, N_TM, stride=N_STN), :][:, column : column + 32]


def settle(t, arrived):
    vmem = pl.BlockSpec(memory_space=pltpu.VMEM)
    return pl.pallas_call(
        settle_kernel,
        out_shape=jax.ShapeDtypeStruct((OWNED, N_TM, BEAMS // N_STN), F32),
        in_specs=[pl.BlockSpec(memory_space=pltpu.SMEM), vmem],
        out_specs=vmem,
        name="settle",
    )(t, arrived)


def across_stations(blocks):
    return lax.all_to_all(blocks, "stn", split_axis=0, concat_axis=0, tiled=True)


def after(value, *others):
    return lax.optimization_barrier((value, *others))[0]


def permuted(block, axis, send_to):
    return lax.ppermute(block, axis, [(i, send_to(i)) for i in range(lax.axis_size(axis))])


def window_round(sums, bits):
    parts = [permuted(sums, "tm", lambda i, flip=flip: i ^ flip) for flip in (bits[0], bits[1], bits[0] | bits[1])]
    return (sums + parts[0]) + (parts[1] + parts[2])


def per_device(voltages, taps, sk_tolerance, station_coords, pointings, station_flags):
    stn = lax.axis_index("stn")
    tm = lax.axis_index("tm")
    me = jnp.reshape(stn, (1,)).astype(jnp.int32)
    table = jnp.asarray(dft_tables())
    perm = jnp.asarray(lane_permutation())
    shift = [(i, i + 1) for i in range(N_TM - 1)]

    visited = np.array(VISITED)
    plans = np.stack([visited, np.array(VISITED_SLOTS), np.array(ORDER), visited // OWNED, visited % OWNED], 1)
    plan = lax.dynamic_index_in_dim(jnp.asarray(plans.astype(np.int32)), stn, 0, False)
    channels, slots, order, owners, places = plan
    offsets = station_coords[:, 0:1] * pointings[None, :, 0] + station_coords[:, 1:2] * pointings[None, :, 1]
    live = (1 - station_flags).astype(F32) * (1.0 / math.sqrt(STATIONS))
    gain = jnp.broadcast_to(live[:, None], (STATIONS, BEAMS))

    (leaving0,) = channelize(voltages, taps, table, 0)
    received0 = lax.ppermute(leaving0, "tm", shift)
    partner = permuted(after(sk_tolerance, leaving0), "tm", lambda i: i ^ WINDOW)
    holder = jnp.arange(CHAN, dtype=jnp.int32) // OWNED
    tolerances = jnp.where(holder == tm, jnp.tile(sk_tolerance, N_TM), 0.0)
    tolerances = jnp.where(holder == (tm ^ WINDOW), jnp.tile(partner, N_TM), tolerances)
    tolerances = jnp.pad(tolerances.reshape(CHAN // 128, 128), ((0, LOCAL_CHAN - CHAN // 128), (0, 0)))

    (leaving1,) = channelize(after(voltages, leaving0), taps, table, 1)
    received1 = lax.ppermute(leaving1, "tm", shift)
    blocks0, sums0 = channelize(after(voltages, leaving1, tolerances), taps, table, 0, received0, me)
    arrived0 = across_stations(blocks0)
    blocks1, sums = channelize(after(voltages, blocks0), taps, table, 1, received1, me, sums0, tolerances)
    weights = steering(after(owners, blocks1), places, offsets, gain)
    arrived1 = across_stations(after(blocks1, weights))

    sums = window_round(after(sums, arrived0, weights), (1, 2))
    sums = window_round(sums, (4, 8))
    tolerance = sums[N_STN, : CHAN // 128].reshape(CHAN)
    window = [sums[0]] + [
        permuted(sums[d], "stn", lambda i, d=d: (i + d) % N_STN) for d in range(1, N_STN)
    ]
    first = gather(arrived0, perm)
    outgoing = beams(me, channels, slots, order, tolerance, window, first, arrived1, perm, weights)
    outgoing = outgoing.reshape(N_TM * N_STN, 1, 128)
    landed = lax.all_to_all(outgoing, ("tm", "stn"), split_axis=0, concat_axis=0, tiled=True)
    return settle(jnp.reshape(tm, (1,)).astype(jnp.int32), landed.reshape(N_TM * N_STN, 128))


def solution(mesh):
    in_specs = (P("tm", None, None, "stn", None), P(), P("tm"), P(), P(), P())
    out_specs = P("tm", None, "stn")
    return jax.shard_map(
        per_device, mesh=mesh, in_specs=in_specs, out_specs=out_specs, check_vma=False
    )
```

profile of v0, /device:TPU:1, one launch (start us, length us, event | category | flops | bytes accessed | tf_op | source)
XLA Modules:
  0.0 155.1 jit_solution(9856997775857294116)
XLA Ops:
  0.9 9.2 %carried.2 = bf16[8,4,96,128]{3,2,1,0:T(8,128)(2,1)} custom-call(bf16[16,2,2,32,2048]{4,3,2,1,0:T(8,128)(2,1)} %refs_4_.5, bf16[16,2,2,32,2048]{4,3,2,1,0:T(8,128)(2,1)} %refs_4_.5, bf16[16,2,2,32,2048]{4,3,2,1,0:T(8,128)(2,1)} %refs_4_.5, bf16[16,2,2,32,2048]{4,3,2,1,0:T(8,128)(2,1)} %refs_4_.5, f32[16,2048]{1,0:T(8,128)S(1)} %copy-done.6, ...), custom_call_target="tpu_custom_call" | custom-call | flops 12000000000 | bytes 8000000 | tf_op jit(solution)/shard_map/carried/pallas_call | solution.py:237
  10.1 4.6 %collective-permute-start.1 = (bf16[8,4,96,128]{3,2,1,0:T(8,128)(2,1)}, bf16[8,4,96,128]{3,2,1,0:T(8,128)(2,1)S(1)}, u32[]{:S(2)}, u32[]{:S(2)}) collective-permute-start(bf16[8,4,96,128]{3,2,1,0:T(8,128)(2,1)} %carried.2), channel_id=1, source_target_pairs={{0,1},{1,2},{2,3},{3,4},{4,5},{5,6},{6,7},{7,8},{8,9},{9,10},{10,1... | collective-permute-start | bytes 2359304 | tf_op jit(solution)/shard_map/ppermute | solution.py:515
  14.8 3.0 %collective-permute-start = (f32[12]{0:T(128)S(1)}, f32[12]{0:T(128)S(1)}, u32[]{:S(2)}, u32[]{:S(2)}) collective-permute-start(f32[12]{0:T(128)S(1)} %copy-done.13), channel_id=1, source_target_pairs={{0,16},{1,17},{2,18},{3,19},{4,20},{5,21},{6,22},{7,23},{8,24},{9,... | collective-permute-start | bytes 152 | tf_op jit(solution)/shard_map/ppermute | solution.py:490
  17.8 8.3 %carried.3 = bf16[8,4,96,128]{3,2,1,0:T(8,128)(2,1)S(1)} custom-call(bf16[16,2,2,32,2048]{4,3,2,1,0:T(8,128)(2,1)} %refs_4_.5, bf16[16,2,2,32,2048]{4,3,2,1,0:T(8,128)(2,1)} %refs_4_.5, bf16[16,2,2,32,2048]{4,3,2,1,0:T(8,128)(2,1)} %refs_4_.5, bf16[16,2,2,32,2048]{4,3,2,1,0:T(8,128)(2,1)} %refs_4_.5, f32[16,2048]{1,0:T(8,128)S(1)} %copy-done.6, ...), custom_call_target="tpu_custom_call" | custom-call | flops 12000000000 | bytes 8000000 | tf_op jit(solution)/shard_map/carried/pallas_call | solution.py:237
  26.1 2.2 %collective-permute-start.2 = (bf16[8,4,96,128]{3,2,1,0:T(8,128)(2,1)S(1)}, bf16[8,4,96,128]{3,2,1,0:T(8,128)(2,1)S(1)}, u32[]{:S(2)}, u32[]{:S(2)}) collective-permute-start(bf16[8,4,96,128]{3,2,1,0:T(8,128)(2,1)S(1)} %carried.3), channel_id=1, source_target_pairs={{0,1},{1,2},{2,3},{3,4},{4,5},{5,6},{6,7},{7,8},{8,9},{9,10},{10,1... | collective-permute-start | bytes 2359304 | tf_op jit(solution)/shard_map/ppermute | solution.py:523
  29.9 9.8 %own.2 = (bf16[8,4,96,128]{3,2,1,0:T(8,128)(2,1)}, f32[8,2,48,128]{3,2,1,0:T(8,128)S(1)}) custom-call(s32[1]{0:T(128)} %bitcast.1.refs_0_.me_ref, bf16[16,2,2,32,2048]{4,3,2,1,0:T(8,128)(2,1)} %refs_4_.5, bf16[16,2,2,32,2048]{4,3,2,1,0:T(8,128)(2,1)} %refs_4_.5, bf16[16,2,2,32,2048]{4,3,2,1,0:T(8,128)(2,1)} %refs_4_.5, ...), custom_call_target="tpu_custom_call" | custom-call | flops 12000000000 | bytes 8000000 | tf_op jit(solution)/shard_map/own/pallas_call | solution.py:237
  40.5 8.2 %all-to-all-start = ((bf16[8,4,96,128]{3,2,1,0:T(8,128)(2,1)}), bf16[8,4,96,128]{3,2,1,0:T(8,128)(2,1)S(1)}, u32[]{:S(2)}, u32[]{:S(2)}) async-start(bf16[8,4,96,128]{3,2,1,0:T(8,128)(2,1)} %get-tuple-element.19), calls=%async_computation | async-start | bytes 1572864 | tf_op jit(solution)/shard_map/all_to_all | solution.py:482
  50.5 9.3 %own.3 = (bf16[8,4,96,128]{3,2,1,0:T(8,128)(2,1)S(1)}, f32[9,48,128]{2,1,0:T(8,128)S(1)}) custom-call(s32[1]{0:T(128)} %bitcast.1.refs_0_.me_ref, bf16[16,2,2,32,2048]{4,3,2,1,0:T(8,128)(2,1)} %refs_4_.5, bf16[16,2,2,32,2048]{4,3,2,1,0:T(8,128)(2,1)} %refs_4_.5, bf16[16,2,2,32,2048]{4,3,2,1,0:T(8,128)(2,1)} %refs_4_.5, ...), custom_call_target="tpu_custom_call" | custom-call | flops 12000000000 | bytes 8000000 | tf_op jit(solution)/shard_map/own/pallas_call | solution.py:237
  61.5 10.1 %steering.1.refs_11_ = bf16[48,256,512]{2,1,0:T(8,128)(2,1)} custom-call(s32[48]{0:T(128)} %get-tuple-element.24.t_ref, s32[48]{0:T(128)} %get-tuple-element.35.o_ref, s32[256,256]{1,0:T(8,128)} %multiply_add_fusion.offset_ref, f32[256,256]{1,0:T(8,128)} %broadcast_in_dim.11.gain_ref), custom_call_target="tpu_custom_call" | custom-call | flops 40000 | bytes 12600 | tf_op jit(solution)/shard_map/steering/pallas_call | solution.py:323
  75.3 6.3 %all-to-all-start.1 = ((bf16[8,4,96,128]{3,2,1,0:T(8,128)(2,1)}), bf16[8,4,96,128]{3,2,1,0:T(8,128)(2,1)S(1)}, u32[]{:S(2)}, u32[]{:S(2)}) async-start(bf16[8,4,96,128]{3,2,1,0:T(8,128)(2,1)} %copy-done.5), calls=%async_computation.1 | async-start | bytes 1572864 | tf_op jit(solution)/shard_map/all_to_all | solution.py:482
  81.6 4.2 %collective-permute-done.5 = f32[9,48,128]{2,1,0:T(8,128)} collective-permute-done((f32[9,48,128]{2,1,0:T(8,128)S(1)}, f32[9,48,128]{2,1,0:T(8,128)}, u32[]{:S(2)}, u32[]{:S(2)}) %collective-permute-start.5) | collective-permute-done | bytes 221216 | tf_op jit(solution)/shard_map/ppermute | solution.py:490
  86.9 2.6 %collective-permute-start.6 = (f32[9,48,128]{2,1,0:T(8,128)S(1)}, f32[9,48,128]{2,1,0:T(8,128)S(1)}, u32[]{:S(2)}, u32[]{:S(2)}) collective-permute-start(f32[9,48,128]{2,1,0:T(8,128)S(1)} %add_add_fusion.1), channel_id=1, source_target_pairs={{0,4},{1,5},{2,6},{3,7},{4,0},{5,1},{6,2},{7,3},{8,12},{9,13},{10,... | collective-permute-start | bytes 663560 | tf_op jit(solution)/shard_map/ppermute | solution.py:490
  91.2 4.3 %collective-permute-done.6 = f32[9,48,128]{2,1,0:T(8,128)S(1)} collective-permute-done((f32[9,48,128]{2,1,0:T(8,128)S(1)}, f32[9,48,128]{2,1,0:T(8,128)S(1)}, u32[]{:S(2)}, u32[]{:S(2)}) %collective-permute-start.6) | collective-permute-done | bytes 221216 | tf_op jit(solution)/shard_map/ppermute | solution.py:490
  96.6 3.7 %collective-permute-done.8 = f32[9,48,128]{2,1,0:T(8,128)S(1)} collective-permute-done((f32[9,48,128]{2,1,0:T(8,128)S(1)}, f32[9,48,128]{2,1,0:T(8,128)S(1)}, u32[]{:S(2)}, u32[]{:S(2)}) %collective-permute-start.8) | collective-permute-done | bytes 221216 | tf_op jit(solution)/shard_map/ppermute | solution.py:490
  100.5 2.0 %collective-permute-start.10 = (f32[48,128]{1,0:T(8,128)S(1)}, f32[48,128]{1,0:T(8,128)S(1)}, u32[]{:S(2)}, u32[]{:S(2)}) collective-permute-start(f32[48,128]{1,0:T(8,128)S(1)} %get-tuple-element.32), channel_id=1, source_target_pairs={{0,64},{32,96},{64,128},{96,160},{128,192},{160,224},{192,0},{224,... | collective-permute-start | bytes 73736 | tf_op jit(solution)/shard_map/ppermute | solution.py:490
  102.5 3.3 %collective-permute-start.11 = (f32[48,128]{1,0:T(8,128)S(1)}, f32[48,128]{1,0:T(8,128)S(1)}, u32[]{:S(2)}, u32[]{:S(2)}) collective-permute-start(f32[48,128]{1,0:T(8,128)S(1)} %get-tuple-element.31), channel_id=1, source_target_pairs={{0,96},{32,128},{64,160},{96,192},{128,224},{160,0},{192,32},{224,... | collective-permute-start | bytes 73736 | tf_op jit(solution)/shard_map/ppermute | solution.py:490
  105.8 1.5 stations.1.refs_8_
  109.7 3.3 %collective-permute-start.13 = (f32[48,128]{1,0:T(8,128)S(1)}, f32[48,128]{1,0:T(8,128)S(1)}, u32[]{:S(2)}, u32[]{:S(2)}) collective-permute-start(f32[48,128]{1,0:T(8,128)S(1)} %get-tuple-element.29), channel_id=1, source_target_pairs={{0,160},{32,192},{64,224},{96,0},{128,32},{160,64},{192,96},{224,1... | collective-permute-start | bytes 73736 | tf_op jit(solution)/shard_map/ppermute | solution.py:490
  113.0 3.3 %collective-permute-start.14 = (f32[48,128]{1,0:T(8,128)S(1)}, f32[48,128]{1,0:T(8,128)S(1)}, u32[]{:S(2)}, u32[]{:S(2)}) collective-permute-start(f32[48,128]{1,0:T(8,128)S(1)} %get-tuple-element.28), channel_id=1, source_target_pairs={{0,192},{32,224},{64,0},{96,32},{128,64},{160,96},{192,128},{224,1... | collective-permute-start | bytes 73736 | tf_op jit(solution)/shard_map/ppermute | solution.py:490
  116.3 1.5 collective-permute-start.9
  120.4 1.4 copy-done.2
  121.8 7.7 %beams.1 = f32[32,8,128]{2,1,0:T(8,128)S(1)} custom-call(s32[1]{0:T(128)} %bitcast.1.refs_0_.me_ref, s32[48]{0:T(128)S(1)} %get-tuple-element.39.chan_ref, s32[48]{0:T(128)S(1)} %get-tuple-element.38.slot_ref, s32[48]{0:T(128)S(1)} %get-tuple-element.37.order_ref, f32[384]{0:T(512)S(1)} %slice_bitcast_fusion.8.tol_ref, ...), custom_call_target="tpu_custom_call" | custom-call | flops 2400000000 | bytes 16000000 | tf_op jit(solution)/shard_map/beams/pallas_call | solution.py:442
  129.5 23.9 %all_to_all.15 = f32[256,1,128]{2,1,0:T(1,128)} all-to-all(f32[256,1,128]{2,1,0:T(1,128)S(1)} %bitcast.38), channel_id=1, replica_groups=mesh['stn'=8,'tm'=32] {'tm','stn'}, dimensions={0} | all-to-all | bytes 262144 | tf_op jit(solution)/shard_map/all_to_all | solution.py:539
  153.4 1.7 %settle.1 = f32[12,32,32]{2,1,0:T(8,128)} custom-call(s32[1]{0:T(128)} %bitcast.t_ref, f32[256,128]{1,0:T(8,128)} %bitcast.39), custom_call_target="tpu_custom_call" | custom-call | tf_op jit(solution)/shard_map/settle/pallas_call | solution.py:472
  (66 shorter events, 19.4 us)
Async XLA Ops:
  10.1 18.2 %copy-start.10 = (s32[256,2]{0,1:T(2,128)S(1)}, s32[256,2]{0,1:T(2,128)}, u32[]{:S(2)}) copy-start(s32[256,2]{0,1:T(2,128)} %param.13) | copy-start | bytes 6148
  10.1 19.0 %copy-start.11 = (s32[256,2]{0,1:T(2,128)S(1)}, s32[256,2]{0,1:T(2,128)}, u32[]{:S(2)}) copy-start(s32[256,2]{0,1:T(2,128)} %param.12) | copy-start | bytes 6148
  10.1 19.8 %copy-start.7 = (f32[16,2048]{1,0:T(8,128)S(1)}, f32[16,2048]{1,0:T(8,128)}, u32[]{:S(2)}) copy-start(f32[16,2048]{1,0:T(8,128)} %refs_8_.5) | copy-start | bytes 393220
  10.1 19.8 %collective-permute-start.1 = (bf16[8,4,96,128]{3,2,1,0:T(8,128)(2,1)}, bf16[8,4,96,128]{3,2,1,0:T(8,128)(2,1)S(1)}, u32[]{:S(2)}, u32[]{:S(2)}) collective-permute-start(bf16[8,4,96,128]{3,2,1,0:T(8,128)(2,1)} %carried.2), channel_id=1, source_target_pairs={{0,1},{1,2},{2,3},{3,4},{4,5},{5,6},{6,7},{7,8},{8,9},{9,10},{10,1... | collective-permute-start | bytes 2359304 | tf_op jit(solution)/shard_map/ppermute | solution.py:515
  14.8 14.9 %collective-permute-start = (f32[12]{0:T(128)S(1)}, f32[12]{0:T(128)S(1)}, u32[]{:S(2)}, u32[]{:S(2)}) collective-permute-start(f32[12]{0:T(128)S(1)} %copy-done.13), channel_id=1, source_target_pairs={{0,16},{1,17},{2,18},{3,19},{4,20},{5,21},{6,22},{7,23},{8,24},{9,... | collective-permute-start | bytes 152 | tf_op jit(solution)/shard_map/ppermute | solution.py:490
  26.1 23.4 %collective-permute-start.2 = (bf16[8,4,96,128]{3,2,1,0:T(8,128)(2,1)S(1)}, bf16[8,4,96,128]{3,2,1,0:T(8,128)(2,1)S(1)}, u32[]{:S(2)}, u32[]{:S(2)}) collective-permute-start(bf16[8,4,96,128]{3,2,1,0:T(8,128)(2,1)S(1)} %carried.3), channel_id=1, source_target_pairs={{0,1},{1,2},{2,3},{3,4},{4,5},{5,6},{6,7},{7,8},{8,9},{9,10},{10,1... | collective-permute-start | bytes 2359304 | tf_op jit(solution)/shard_map/ppermute | solution.py:523
  29.9 18.8 %copy-start.12 = (s32[256]{0:T(256)S(1)}, s32[256]{0:T(256)}, u32[]{:S(2)}) copy-start(s32[256]{0:T(256)} %param.14) | copy-start | bytes 3076
  40.5 31.8 %all-to-all-start = ((bf16[8,4,96,128]{3,2,1,0:T(8,128)(2,1)}), bf16[8,4,96,128]{3,2,1,0:T(8,128)(2,1)S(1)}, u32[]{:S(2)}, u32[]{:S(2)}) async-start(bf16[8,4,96,128]{3,2,1,0:T(8,128)(2,1)} %get-tuple-element.19), calls=%async_computation | async-start | bytes 1572864 | tf_op jit(solution)/shard_map/all_to_all | solution.py:482
  71.6 34.2 %copy-start = (bf16[1024,1024]{1,0:T(8,128)(2,1)S(1)}, bf16[1024,1024]{1,0:T(8,128)(2,1)}, u32[]{:S(2)}) copy-start(bf16[1024,1024]{1,0:T(8,128)(2,1)} %constant.45.clone.perm_ref.refs_10_) | copy-start | bytes 6291460
  73.1 8.5 %collective-permute-start.3 = (f32[9,48,128]{2,1,0:T(8,128)S(1)}, f32[9,48,128]{2,1,0:T(8,128)S(1)}, u32[]{:S(2)}, u32[]{:S(2)}) collective-permute-start(f32[9,48,128]{2,1,0:T(8,128)S(1)} %get-tuple-element.25), channel_id=1, source_target_pairs={{0,1},{1,0},{2,3},{3,2},{4,5},{5,4},{6,7},{7,6},{8,9},{9,8},{10,11... | collective-permute-start | bytes 663560 | tf_op jit(solution)/shard_map/ppermute | solution.py:490
  73.6 8.0 %collective-permute-start.4 = (f32[9,48,128]{2,1,0:T(8,128)S(1)}, f32[9,48,128]{2,1,0:T(8,128)}, u32[]{:S(2)}, u32[]{:S(2)}) collective-permute-start(f32[9,48,128]{2,1,0:T(8,128)S(1)} %get-tuple-element.25), channel_id=1, source_target_pairs={{0,2},{1,3},{2,0},{3,1},{4,6},{5,7},{6,4},{7,5},{8,10},{9,11},{10,... | collective-permute-start | bytes 663560 | tf_op jit(solution)/shard_map/ppermute | solution.py:490
  74.9 10.9 %collective-permute-start.5 = (f32[9,48,128]{2,1,0:T(8,128)S(1)}, f32[9,48,128]{2,1,0:T(8,128)}, u32[]{:S(2)}, u32[]{:S(2)}) collective-permute-start(f32[9,48,128]{2,1,0:T(8,128)S(1)} %get-tuple-element.25), channel_id=1, source_target_pairs={{0,3},{1,2},{2,1},{3,0},{4,7},{5,6},{6,5},{7,4},{8,11},{9,10},{10,... | collective-permute-start | bytes 663560 | tf_op jit(solution)/shard_map/ppermute | solution.py:490
  75.3 42.5 %all-to-all-start.1 = ((bf16[8,4,96,128]{3,2,1,0:T(8,128)(2,1)}), bf16[8,4,96,128]{3,2,1,0:T(8,128)(2,1)S(1)}, u32[]{:S(2)}, u32[]{:S(2)}) async-start(bf16[8,4,96,128]{3,2,1,0:T(8,128)(2,1)} %copy-done.5), calls=%async_computation.1 | async-start | bytes 1572864 | tf_op jit(solution)/shard_map/all_to_all | solution.py:482
  81.6 24.2 %copy-start.4 = (bf16[8,4,96,128]{3,2,1,0:T(8,128)(2,1)S(1)}, bf16[8,4,96,128]{3,2,1,0:T(8,128)(2,1)}, u32[]{:S(2)}) copy-start(bf16[8,4,96,128]{3,2,1,0:T(8,128)(2,1)} %copy-done.3) | copy-start | bytes 2359300
  86.9 8.6 %collective-permute-start.6 = (f32[9,48,128]{2,1,0:T(8,128)S(1)}, f32[9,48,128]{2,1,0:T(8,128)S(1)}, u32[]{:S(2)}, u32[]{:S(2)}) collective-permute-start(f32[9,48,128]{2,1,0:T(8,128)S(1)} %add_add_fusion.1), channel_id=1, source_target_pairs={{0,4},{1,5},{2,6},{3,7},{4,0},{5,1},{6,2},{7,3},{8,12},{9,13},{10,... | collective-permute-start | bytes 663560 | tf_op jit(solution)/shard_map/ppermute | solution.py:490
  89.5 7.1 %collective-permute-start.7 = (f32[9,48,128]{2,1,0:T(8,128)S(1)}, f32[9,48,128]{2,1,0:T(8,128)S(1)}, u32[]{:S(2)}, u32[]{:S(2)}) collective-permute-start(f32[9,48,128]{2,1,0:T(8,128)S(1)} %add_add_fusion.1), channel_id=1, source_target_pairs={{0,8},{1,9},{2,10},{3,11},{4,12},{5,13},{6,14},{7,15},{8,0},{9,1},... | collective-permute-start | bytes 663560 | tf_op jit(solution)/shard_map/ppermute | solution.py:490
  89.9 10.5 %collective-permute-start.8 = (f32[9,48,128]{2,1,0:T(8,128)S(1)}, f32[9,48,128]{2,1,0:T(8,128)S(1)}, u32[]{:S(2)}, u32[]{:S(2)}) collective-permute-start(f32[9,48,128]{2,1,0:T(8,128)S(1)} %add_add_fusion.1), channel_id=1, source_target_pairs={{0,12},{1,13},{2,14},{3,15},{4,8},{5,9},{6,10},{7,11},{8,4},{9,5},... | collective-permute-start | bytes 663560 | tf_op jit(solution)/shard_map/ppermute | solution.py:490
  100.5 15.8 %collective-permute-start.10 = (f32[48,128]{1,0:T(8,128)S(1)}, f32[48,128]{1,0:T(8,128)S(1)}, u32[]{:S(2)}, u32[]{:S(2)}) collective-permute-start(f32[48,128]{1,0:T(8,128)S(1)} %get-tuple-element.32), channel_id=1, source_target_pairs={{0,64},{32,96},{64,128},{96,160},{128,192},{160,224},{192,0},{224,... | collective-permute-start | bytes 73736 | tf_op jit(solution)/shard_map/ppermute | solution.py:490
  102.5 13.8 %collective-permute-start.11 = (f32[48,128]{1,0:T(8,128)S(1)}, f32[48,128]{1,0:T(8,128)S(1)}, u32[]{:S(2)}, u32[]{:S(2)}) collective-permute-start(f32[48,128]{1,0:T(8,128)S(1)} %get-tuple-element.31), channel_id=1, source_target_pairs={{0,96},{32,128},{64,160},{96,192},{128,224},{160,0},{192,32},{224,... | collective-permute-start | bytes 73736 | tf_op jit(solution)/shard_map/ppermute | solution.py:490
  108.5 9.2 %collective-permute-start.12 = (f32[48,128]{1,0:T(8,128)S(1)}, f32[48,128]{1,0:T(8,128)S(1)}, u32[]{:S(2)}, u32[]{:S(2)}) collective-permute-start(f32[48,128]{1,0:T(8,128)S(1)} %get-tuple-element.30), channel_id=1, source_target_pairs={{0,128},{32,160},{64,192},{96,224},{128,0},{160,32},{192,64},{224,... | collective-permute-start | bytes 73736 | tf_op jit(solution)/shard_map/ppermute | solution.py:490
  109.7 8.1 %collective-permute-start.13 = (f32[48,128]{1,0:T(8,128)S(1)}, f32[48,128]{1,0:T(8,128)S(1)}, u32[]{:S(2)}, u32[]{:S(2)}) collective-permute-start(f32[48,128]{1,0:T(8,128)S(1)} %get-tuple-element.29), channel_id=1, source_target_pairs={{0,160},{32,192},{64,224},{96,0},{128,32},{160,64},{192,96},{224,1... | collective-permute-start | bytes 73736 | tf_op jit(solution)/shard_map/ppermute | solution.py:490
  113.0 4.8 %collective-permute-start.14 = (f32[48,128]{1,0:T(8,128)S(1)}, f32[48,128]{1,0:T(8,128)S(1)}, u32[]{:S(2)}, u32[]{:S(2)}) collective-permute-start(f32[48,128]{1,0:T(8,128)S(1)} %get-tuple-element.28), channel_id=1, source_target_pairs={{0,192},{32,224},{64,0},{96,32},{128,64},{160,96},{192,128},{224,1... | collective-permute-start | bytes 73736 | tf_op jit(solution)/shard_map/ppermute | solution.py:490
  116.3 2.8 %collective-permute-start.15 = (f32[48,128]{1,0:T(8,128)S(1)}, f32[48,128]{1,0:T(8,128)S(1)}, u32[]{:S(2)}, u32[]{:S(2)}) collective-permute-start(f32[48,128]{1,0:T(8,128)S(1)} %get-tuple-element.27), channel_id=1, source_target_pairs={{0,224},{32,0},{64,32},{96,64},{128,96},{160,128},{192,160},{224,1... | collective-permute-start | bytes 73736 | tf_op jit(solution)/shard_map/ppermute | solution.py:490
  116.3 4.1 %collective-permute-start.9 = (f32[48,128]{1,0:T(8,128)S(1)}, f32[48,128]{1,0:T(8,128)S(1)}, u32[]{:S(2)}, u32[]{:S(2)}) collective-permute-start(f32[48,128]{1,0:T(8,128)S(1)} %get-tuple-element.33), channel_id=1, source_target_pairs={{0,32},{32,64},{64,96},{96,128},{128,160},{160,192},{192,224},{224... | collective-permute-start | bytes 73736 | tf_op jit(solution)/shard_map/ppermute | solution.py:490
  (8 other events, 20.9 us)
where the time goes:
time: 156 us; the launch traced here: 155 us
  Pallas kernels  57.6 us (37%)
  starting transfers between devices  45.3 us (29%)
  blocking collectives  23.9 us (15%)
  waiting for transfers between devices  16.7 us (11%)
  local copies, waits for them, and re-layouts  9.33 us (6%)
  other arithmetic  2.03 us (1%)
    pallas_call x4, Pallas kernels, channelize(): pl.pallas_call(functools.partial(channelize_kernel, carried, polar), out_...  36.6 us
    ppermute x14, starting transfers between devices, permuted(): lax.ppermute(block, axis, [(i, send_to(i)) for i in range(lax.axis_size(a...  24 us
    all_to_all x1, blocking collectives, per_device(): lax.all_to_all(outgoing, ('tm', 'stn'), split_axis=0, concat_axis=0, tile...  23.9 us
    ppermute x14, waiting for transfers between devices, permuted(): lax.ppermute(block, axis, [(i, send_to(i)) for i in range(lax.axis_size(a...  16.1 us
    all_to_all x2, starting transfers between devices, across_stations(): lax.all_to_all(blocks, 'stn', split_axis=0, concat_axis=0, tiled=True)  14.5 us
    pallas_call x1, Pallas kernels, steering(): pl.pallas_call(steering_kernel, out_shape=jax.ShapeDtypeStruct((LOCAL_CHA...  10.1 us
    pallas_call x1, Pallas kernels, beams(): pl.pallas_call(beam_kernel, out_shape=jax.ShapeDtypeStruct((N_TM, N_STN,...  7.74 us
    unnamed x28, local copies, waits for them, and re-layouts  7.01 us
  transfers between devices with their start and end apart: 18, of which 7 were waited for; matrix products, arithmetic and copies ran while one was open for 3% of the time, Pallas kernels for 25%

commit v1 on v0

v1 whole, which is shorter than its diff:
```python
import functools
import math

import jax
import jax.numpy as jnp
import numpy as np
from jax import lax
from jax.experimental import pallas as pl
from jax.experimental.pallas import tpu as pltpu
from jax.sharding import PartitionSpec as P

STATIONS = 256
NFFT = 2048
CHAN = 384
BEAMS = 256
INTEG = 16
TAPS = 16
FRAMES = 16
N_STN = 8
N_TM = 32
S_DEV = 32
LOCAL_CHAN = CHAN // N_STN
OWNED = CHAN // N_TM
WINDOW = 16
RADIX = 4
POINTS = NFFT // RADIX
SEGS = 4
F32 = jnp.float32
BF16 = jnp.bfloat16

EVEN = (0, 4, 1, 5, 10, 11)
ODD = (2, 6, 3, 7, 8, 9)


def stn_of(offset, t):
    if offset in EVEN:
        return 2 * ((EVEN.index(offset) + t) % 4)
    return 2 * ((ODD.index(offset) + t) % 4) + 1


def slot_of(offset):
    return 1 if offset >= 8 else 0


def channel_plan():
    channels, slots, sizes = [], [], []
    for k in range(N_STN):
        mine, places, count = [], [], []
        for residue in range(RADIX):
            before = len(mine)
            for t in range(N_TM):
                for offset in range(residue, OWNED, RADIX):
                    if stn_of(offset, t) == k:
                        mine.append(OWNED * t + offset)
                        places.append(N_TM * slot_of(offset) + t)
            count.append(len(mine) - before)
        assert len(mine) == LOCAL_CHAN and len(set(places)) == LOCAL_CHAN
        assert all(n % 8 == 0 for n in count)
        channels.append(mine)
        slots.append(places)
        sizes.append(count)
    return channels, slots, sizes


CHANNELS, SLOTS, SIZES = channel_plan()
ORDER = [sorted(range(LOCAL_CHAN), key=lambda n, mine=mine: mine[n]) for mine in CHANNELS]
VISITED = [[mine[n] for n in order] for mine, order in zip(CHANNELS, ORDER)]
assert all(c // OWNED // (N_TM // 2) == n // (LOCAL_CHAN // 2) for mine in VISITED for n, c in enumerate(mine))
VISITED_SLOTS = [[places[n] for n in order] for places, order in zip(SLOTS, ORDER)]


def dft_tables():
    tables = []
    points = np.arange(POINTS)
    for residue in range(RADIX):
        order = []
        for k in range(N_STN):
            start = sum(SIZES[k][:residue])
            order += CHANNELS[k][start : start + SIZES[k][residue]]
        turns = (np.array(order)[:, None] * points[None, :]) % NFFT
        angle = 2.0 * np.pi * turns / NFFT
        cosine = np.cos(angle) / math.sqrt(NFFT)
        sine = np.sin(angle) / math.sqrt(NFFT)
        real_rows = np.stack([cosine, sine], 1)
        imag_rows = np.stack([-sine, cosine], 1)
        columns = np.zeros((2 * POINTS, 256))
        for part, rows in enumerate((real_rows, imag_rows)):
            rows = rows.reshape(-1, 2, POINTS // 128, 128).transpose(2, 1, 3, 0)
            columns[:, 128 * part : 128 * part + CHAN // RADIX] = rows.reshape(2 * POINTS, -1)
        tables.append(columns)
    return np.stack(tables, 0).astype(np.float32).astype(jnp.bfloat16)


def lane_permutation():
    source = np.arange(N_STN * 128)
    d, f4, s = source // 128, source // 32 % 4, source % 32
    target = f4 * STATIONS + d * S_DEV + s
    onehot = np.zeros((N_STN * 128, 4 * STATIONS), np.float32)
    onehot[source, target] = 1.0
    return onehot.astype(jnp.bfloat16)


ROWS = FRAMES * S_DEV


def channelize_kernel(carried, *refs):
    v_refs, tap_refs, table_ref, out_ref = refs[:RADIX], refs[RADIX : 2 * RADIX], refs[2 * RADIX], refs[2 * RADIX + 1]
    mixed, filtered, spectra, tables, arrival = refs[2 * RADIX + 2 :]
    step = pl.program_id(0)
    outputs = FRAMES - 1 if carried else FRAMES
    load = pltpu.make_async_copy(table_ref, tables, arrival)

    @pl.when(step == 0)
    def _():
        load.start()

    def rows_chunk(chunk, _):
        polar = chunk // 2
        row = pl.multiple_of(chunk % 2 * 16, 16)
        for j in range(RADIX):
            taps = [jnp.broadcast_to(tap_refs[j][k : k + 1, :], (16, 128)) for k in range(TAPS)]
            for r in range(2):
                x = [v_refs[j][f, r, polar, pl.ds(row, 16), :].astype(F32) for f in range(FRAMES)]
                for g in range(outputs):
                    if carried:
                        pairs = [(k, FRAMES + g - k) for k in range(g + 1, TAPS)]
                    else:
                        pairs = [(k, g - k) for k in range(g + 1)]
                    total = taps[pairs[0][0]] * x[pairs[0][1]]
                    for k, f in pairs[1:]:
                        total = total + taps[k] * x[f]
                    filtered[r, j, g] = total
        column = pl.multiple_of(step * 256, 256)
        for g in range(outputs):
            re = [filtered[0, j, g] for j in range(RADIX)]
            im = [filtered[1, j, g] for j in range(RADIX)]
            ar, ai = re[0] + re[2], im[0] + im[2]
            br, bi = re[0] - re[2], im[0] - im[2]
            cr, ci = re[1] + re[3], im[1] + im[3]
            dr, di = re[1] - re[3], im[1] - im[3]
            parts = (
                (ar + cr, ai + ci),
                (br + di, bi - dr),
                (ar - cr, ai - ci),
                (br - di, bi + dr),
            )
            target = pl.multiple_of(polar * ROWS + g * S_DEV + row, 16)
            for residue, (y_re, y_im) in enumerate(parts):
                mixed[residue, pl.ds(target, 16), pl.ds(column, 128)] = y_re.astype(BF16)
                mixed[residue, pl.ds(target, 16), pl.ds(column + 128, 128)] = y_im.astype(BF16)
        return 0

    lax.fori_loop(0, 2 * (S_DEV // 16), rows_chunk, 0)

    @pl.when(step == pl.num_programs(0) - 1)
    def _():
        load.wait()
        if carried:
            for residue in range(RADIX):
                for polar in range(2):
                    last = polar * ROWS + outputs * S_DEV
                    mixed[residue, last : last + S_DEV, :] = jnp.zeros((S_DEV, 2 * POINTS), BF16)
        for residue in range(RADIX):
            product = jnp.dot(mixed[residue], tables[residue], preferred_element_type=F32)
            for seg in range(2 * SEGS):
                rows = product[seg * 128 : seg * 128 + 128]
                spectra[residue, 0, seg] = rows[:, :128].T
                spectra[residue, 1, seg] = rows[:, 128:].T
        for k in range(N_STN):
            rows = [sum(SIZES[n][residue] for n in range(k)) for residue in range(RADIX)]
            for seg in range(2 * SEGS):
                for part in range(2):
                    piece = jnp.concatenate(
                        [
                            spectra[residue, part, seg, rows[residue] : rows[residue] + SIZES[k][residue]]
                            for residue in range(RADIX)
                        ],
                        0,
                    )
                    at = slice(part * LOCAL_CHAN, (part + 1) * LOCAL_CHAN)
                    out_ref[k, seg, at] = piece.astype(out_ref.dtype)


BLOCKS = (N_STN, 2 * SEGS, 2 * LOCAL_CHAN, 128)


def channelize(voltages, taps, table, carried):
    steps = POINTS // 128
    v_specs = [
        pl.BlockSpec((FRAMES, 2, 2, S_DEV, 128), functools.partial(lambda j, i: (0, 0, 0, 0, j * steps + i), j))
        for j in range(RADIX)
    ]
    t_specs = [
        pl.BlockSpec((TAPS, 128), functools.partial(lambda j, i: (0, j * steps + i), j)) for j in range(RADIX)
    ]
    voltages, taps, table = (pltpu.with_memory_space_constraint(x, pltpu.HBM) for x in (voltages, taps, table))
    return pl.pallas_call(
        functools.partial(channelize_kernel, carried),
        out_shape=jax.ShapeDtypeStruct(BLOCKS, BF16 if carried else F32),
        grid=(steps,),
        in_specs=v_specs + t_specs + [pl.BlockSpec(memory_space=pl.ANY)],
        out_specs=pl.BlockSpec(memory_space=pltpu.VMEM),
        scratch_shapes=[
            pltpu.VMEM((RADIX, 2 * ROWS, 2 * POINTS), BF16),
            pltpu.VMEM((2, RADIX, FRAMES, 16, 128), F32),
            pltpu.VMEM((RADIX, 2, 2 * SEGS, 128, 128), F32),
            pltpu.VMEM(table.shape, BF16),
            pltpu.SemaphoreType.DMA(()),
        ],
        compiler_params=pltpu.CompilerParams(
            dimension_semantics=("arbitrary",), vmem_limit_bytes=40 * 1024 * 1024
        ),
        cost_estimate=pl.CostEstimate(flops=14_000_000_000, bytes_accessed=16_000_000, transcendentals=0),
        name="carried" if carried else "own",
    )(*([voltages] * RADIX), *([taps] * RADIX), table)


def combine_kernel(me_ref, own_ref, received_ref, tol_ref, out_ref, packed_ref, spectra, leaving):
    lane = lax.broadcasted_iota(jnp.int32, (LOCAL_CHAN, 128), 1)
    for k in range(N_STN):
        packed = None
        for polar in range(2):
            first = second = None
            for seg in range(polar * SEGS, (polar + 1) * SEGS):
                value = (own_ref[k, seg] + received_ref[k, seg].astype(F32)).astype(BF16)
                spectra[k, seg] = value
                value = value.astype(F32)
                power = value[:LOCAL_CHAN] * value[:LOCAL_CHAN] + value[LOCAL_CHAN:] * value[LOCAL_CHAN:]
                square = power * power
                first = power if first is None else first + power
                second = square if second is None else second + square
            for kind, total in enumerate((first, second)):
                total = total + pltpu.roll(total, 64, 1)
                total = total + pltpu.roll(total, 32, 1)
                group = 2 * polar + kind
                packed = total if group == 0 else jnp.where(lane // 32 == group, total, packed)
        pltpu.make_async_copy(spectra.at[k], out_ref.at[k], leaving.at[k]).start()
        packed_ref[lax.rem(k + N_STN - me_ref[0], N_STN)] = packed
    packed_ref[N_STN] = tol_ref[...]
    for k in range(N_STN):
        pltpu.make_async_copy(spectra.at[k], out_ref.at[k], leaving.at[k]).wait()


def combine(me, own, received, tolerances):
    vmem = pl.BlockSpec(memory_space=pltpu.VMEM)
    return pl.pallas_call(
        combine_kernel,
        out_shape=[
            jax.ShapeDtypeStruct(BLOCKS, BF16),
            jax.ShapeDtypeStruct((N_STN + 1, LOCAL_CHAN, 128), F32),
        ],
        in_specs=[pl.BlockSpec(memory_space=pltpu.SMEM), vmem, vmem, vmem],
        out_specs=[pl.BlockSpec(memory_space=pltpu.HBM), vmem],
        scratch_shapes=[pltpu.VMEM(BLOCKS, BF16), pltpu.SemaphoreType.DMA((N_STN,))],
        compiler_params=pltpu.CompilerParams(vmem_limit_bytes=16 * 1024 * 1024),
        cost_estimate=pl.CostEstimate(flops=8_000_000, bytes_accessed=8_000_000, transcendentals=0),
        name="combine",
    )(me, own, received, tolerances)


STATION_ROWS = 32


def turn(offsets, number):
    unit = 2.0 * math.pi / 65536.0
    residue = (offsets * number) & 65535
    quadrant = (residue + 8192) >> 14
    angle = (residue - (quadrant << 14)).astype(F32) * unit
    square = angle * angle
    sine = angle * (1.0 + square * (-1.0 / 6.0 + square * (1.0 / 120.0 - square * (1.0 / 5040.0))))
    cosine = 1.0 + square * (
        -0.5 + square * (1.0 / 24.0 + square * (-1.0 / 720.0 + square * (1.0 / 40320.0)))
    )
    odd = (quadrant & 1) == 1
    real = jnp.where(odd, sine, cosine)
    imag = jnp.where(odd, cosine, sine)
    real = jnp.where(((quadrant + 1) & 2) == 2, -real, real)
    imag = jnp.where((quadrant & 2) == 2, -imag, imag)
    return real, imag


def times(a, b):
    return a[0] * b[0] - a[1] * b[1], a[0] * b[1] + a[1] * b[0]


def steering_kernel(start, t_ref, o_ref, offset_ref, gain_ref, out_ref, coarse, fine):
    offsets = offset_ref[...]
    single = turn(offsets, 1)
    pair = times(single, single)
    fine[0, 0], fine[0, 1] = single
    fine[1, 0], fine[1, 1] = pair
    for o in range(2, OWNED):
        fine[o, 0], fine[o, 1] = times((fine[o - 2, 0], fine[o - 2, 1]), pair)
    stride = (fine[OWNED - 1, 0], fine[OWNED - 1, 1])
    double = times(stride, stride)
    fast = times(double, double)
    gain = gain_ref[...]
    value = (gain, jnp.zeros_like(gain))
    if start:
        value = tuple(part * gain for part in turn(offsets, OWNED * start))
    for t in range(4):
        coarse[t, 0], coarse[t, 1] = value
        if t < 3:
            value = times(value, stride)
    for t in range(4, N_TM // 2):
        coarse[t, 0], coarse[t, 1] = times((coarse[t - 4, 0], coarse[t - 4, 1]), fast)

    def channels(n, _):
        for i in range(4):
            at = 4 * n + i
            t, o = t_ref[at] - start, o_ref[at]
            real, imag = times((coarse[t, 0], coarse[t, 1]), (fine[o, 0], fine[o, 1]))
            out_ref[at, :, :BEAMS] = real.astype(BF16)
            out_ref[at, :, BEAMS:] = imag.astype(BF16)
        return 0

    lax.fori_loop(0, HALF // 4, channels, 0)


HALF = LOCAL_CHAN // 2


def steering(start, owners, places, offsets, gain):
    smem = pl.BlockSpec(memory_space=pltpu.SMEM)
    rows = pl.BlockSpec((STATION_ROWS, BEAMS), lambda i: (i, 0))
    return pl.pallas_call(
        functools.partial(steering_kernel, start),
        out_shape=jax.ShapeDtypeStruct((HALF, STATIONS, 2 * BEAMS), BF16),
        grid=(STATIONS // STATION_ROWS,),
        in_specs=[smem, smem, rows, rows],
        out_specs=pl.BlockSpec((HALF, STATION_ROWS, 2 * BEAMS), lambda i: (0, i, 0)),
        scratch_shapes=[
            pltpu.VMEM((N_TM // 2, 2, STATION_ROWS, BEAMS), F32),
            pltpu.VMEM((OWNED, 2, STATION_ROWS, BEAMS), F32),
        ],
        compiler_params=pltpu.CompilerParams(
            dimension_semantics=("arbitrary",), vmem_limit_bytes=54 * 1024 * 1024
        ),
        cost_estimate=pl.CostEstimate(flops=40_000, bytes_accessed=12_600, transcendentals=0),
        name="steering",
    )(owners, places, offsets, gain)


def place_stations(in_ref, polar, perm_ref, out_ref):
    for seg in range(SEGS):
        stacked = jnp.concatenate([in_ref[g, polar * SEGS + seg] for g in range(N_STN)], 1)
        moved = jnp.dot(stacked, perm_ref[...], preferred_element_type=F32)
        for part in range(2):
            rows = moved[part * LOCAL_CHAN : (part + 1) * LOCAL_CHAN]
            for f4 in range(4):
                at = ((part * 4 + f4) * SEGS + seg) * LOCAL_CHAN
                for half in range(2):
                    column = f4 * STATIONS + half * 128
                    out_ref[half, at : at + LOCAL_CHAN, :] = rows[:, column : column + 128]


PLACED = (2, 32 * LOCAL_CHAN, 128)


BLOCK = 8
CHUNKS = LOCAL_CHAN // BLOCK


def beam_kernel(me_ref, chan_ref, slot_ref, order_ref, tol_ref, *refs):
    sum_refs = refs[:N_STN]
    in_ref, perm_ref, low_ref, high_ref, out_ref = refs[N_STN : N_STN + 5]
    window_sums, ordered, first_placed, second_placed, perm, weights, powers, arrival = refs[N_STN + 5 :]

    def load(chunk):
        source, at = (low_ref, chunk) if chunk < CHUNKS // 2 else (high_ref, chunk - CHUNKS // 2)
        return pltpu.make_async_copy(
            source.at[pl.ds(at * BLOCK, BLOCK)], weights.at[pl.ds(chunk * BLOCK, BLOCK)], arrival.at[chunk]
        )

    load_perm = pltpu.make_async_copy(perm_ref, perm, arrival.at[CHUNKS])
    load_perm.start()
    for chunk in range(CHUNKS):
        load(chunk).start()
    powers[...] = jnp.zeros_like(powers)
    lane = lax.broadcasted_iota(jnp.int32, (LOCAL_CHAN, 128), 1)
    for d in range(N_STN):
        ordered[lax.rem(me_ref[0] + N_STN - d, N_STN)] = sum_refs[d][...]
    for polar in range(2):
        for kind in range(2):
            group = 2 * polar + kind
            for half in range(2):
                total = jnp.zeros((LOCAL_CHAN, 128), F32)
                for place in range(4):
                    shift = 32 * ((place - group) % 4)
                    piece = ordered[4 * half + place]
                    if shift:
                        piece = pltpu.roll(piece, shift, 1)
                    total = jnp.where(lane // 32 == place, piece, total)
                window_sums[polar, kind, :, half * 128 : half * 128 + 128] = total
    load_perm.wait()
    place_stations(in_ref, 0, perm, first_placed)
    place_stations(in_ref, 1, perm, second_placed)

    size = float(WINDOW * FRAMES)

    for chunk in range(CHUNKS):
        load(chunk).wait()
        for inner in range(BLOCK):
            visit = chunk * BLOCK + inner
            local = order_ref[visit]
            tolerance = tol_ref[chan_ref[visit]]
            rows = []
            for polar, ref in enumerate((first_placed, second_placed)):
                s1 = window_sums[polar, 0, pl.ds(local, 1), :]
                s2 = window_sums[polar, 1, pl.ds(local, 1), :]
                kurtosis = (size + 1.0) / (size - 1.0) * (size * s2 / (s1 * s1) - 1.0)
                deviation = (kurtosis - 1.0) / tolerance
                soft = 1.0 / (1.0 + deviation * deviation)
                halves = [ref[half, pl.ds(local, 32, stride=LOCAL_CHAN), :] for half in range(2)]
                values = jnp.concatenate(halves, 1)
                rows.append((values * soft).astype(BF16))
            stacked = jnp.concatenate([rows[0][:16], rows[1][:16], rows[0][16:], rows[1][16:]], 0)
            product = jnp.dot(stacked, weights[visit], preferred_element_type=F32)
            real = product[:32, :BEAMS] - product[32:, BEAMS:]
            imag = product[:32, BEAMS:] + product[32:, :BEAMS]
            power = jnp.sum(real * real + imag * imag, 0, keepdims=True) * (1.0 / (2.0 * INTEG))
            powers[pl.ds(slot_ref[visit], 1), :] = power

    share = BEAMS // N_STN
    out_ref[...] = jnp.zeros_like(out_ref)
    for slot in range(2):
        rows = powers[slot * N_TM : (slot + 1) * N_TM, :]
        for j in range(N_STN):
            out_ref[:, j, slot * share : (slot + 1) * share] = rows[:, j * share : (j + 1) * share]


def beams(me, channels, slots, order, tolerance, sums, arrived, perm, low, high):
    smem = pl.BlockSpec(memory_space=pltpu.SMEM)
    vmem = pl.BlockSpec(memory_space=pltpu.VMEM)
    low, high, perm = (pltpu.with_memory_space_constraint(x, pltpu.HBM) for x in (low, high, perm))
    return pl.pallas_call(
        beam_kernel,
        out_shape=jax.ShapeDtypeStruct((N_TM, N_STN, 128), F32),
        in_specs=[smem] * 5 + [vmem] * (N_STN + 1) + [pl.BlockSpec(memory_space=pl.ANY)] * 3,
        out_specs=vmem,
        scratch_shapes=[
            pltpu.VMEM((2, 2, LOCAL_CHAN, STATIONS), F32),
            pltpu.VMEM((N_STN, LOCAL_CHAN, 128), F32),
            pltpu.VMEM(PLACED, F32),
            pltpu.VMEM(PLACED, F32),
            pltpu.VMEM(perm.shape, BF16),
            pltpu.VMEM((LOCAL_CHAN, STATIONS, 2 * BEAMS), BF16),
            pltpu.VMEM((2 * N_TM, BEAMS), F32),
            pltpu.SemaphoreType.DMA((CHUNKS + 1,)),
        ],
        compiler_params=pltpu.CompilerParams(vmem_limit_bytes=36 * 1024 * 1024),
        cost_estimate=pl.CostEstimate(flops=2_400_000_000, bytes_accessed=16_000_000, transcendentals=0),
        name="beams",
    )(me, channels, slots, order, tolerance, *sums, arrived, perm, low, high)


def settle_kernel(t_ref, in_ref, out_ref):
    for offset in range(OWNED):
        group = EVEN if offset in EVEN else ODD
        parity = 0 if offset in EVEN else 1
        k = 2 * lax.rem(group.index(offset) + t_ref[0], 4) + parity
        column = slot_of(offset) * 32
        out_ref[offset] = in_ref[pl.ds(k, N_TM, stride=N_STN), :][:, column : column + 32]


def settle(t, arrived):
    vmem = pl.BlockSpec(memory_space=pltpu.VMEM)
    return pl.pallas_call(
        settle_kernel,
        out_shape=jax.ShapeDtypeStruct((OWNED, N_TM, BEAMS // N_STN), F32),
        in_specs=[pl.BlockSpec(memory_space=pltpu.SMEM), vmem],
        out_specs=vmem,
        name="settle",
    )(t, arrived)


def across_stations(blocks):
    return lax.all_to_all(blocks, "stn", split_axis=0, concat_axis=0, tiled=True)


def after(value, *others):
    return lax.optimization_barrier((value, *others))[0]


def permuted(block, axis, send_to):
    return lax.ppermute(block, axis, [(i, send_to(i)) for i in range(lax.axis_size(axis))])


def window_round(sums, bits):
    parts = [permuted(sums, "tm", lambda i, flip=flip: i ^ flip) for flip in (bits[0], bits[1], bits[0] | bits[1])]
    return (sums + parts[0]) + (parts[1] + parts[2])


def per_device(voltages, taps, sk_tolerance, station_coords, pointings, station_flags):
    stn = lax.axis_index("stn")
    tm = lax.axis_index("tm")
    me = jnp.reshape(stn, (1,)).astype(jnp.int32)
    table = jnp.asarray(dft_tables())
    perm = jnp.asarray(lane_permutation())
    shift = [(i, i + 1) for i in range(N_TM - 1)]

    visited = np.array(VISITED)
    plans = np.stack([visited, np.array(VISITED_SLOTS), np.array(ORDER), visited // OWNED, visited % OWNED], 1)
    plan = lax.dynamic_index_in_dim(jnp.asarray(plans.astype(np.int32)), stn, 0, False)
    channels, slots, order, owners, places = plan
    offsets = station_coords[:, 0:1] * pointings[None, :, 0] + station_coords[:, 1:2] * pointings[None, :, 1]
    live = (1 - station_flags).astype(F32) * (1.0 / math.sqrt(STATIONS))
    gain = jnp.broadcast_to(live[:, None], (STATIONS, BEAMS))

    leaving = channelize(voltages, taps, table, True)
    received = lax.ppermute(leaving, "tm", shift)
    holder = jnp.arange(CHAN, dtype=jnp.int32) // OWNED
    tolerances = jnp.where(holder == tm, jnp.tile(sk_tolerance, N_TM), 0.0)
    tolerances = jnp.pad(tolerances.reshape(CHAN // 128, 128), ((0, LOCAL_CHAN - CHAN // 128), (0, 0)))

    own = channelize(after(voltages, leaving), taps, table, False)
    blocks, sums = combine(me, own, received, tolerances)
    arrived = across_stations(blocks)
    sums = window_round(sums, (1, 2))
    low = steering(0, after(owners[:HALF], blocks), places[:HALF], offsets, gain)
    sums = window_round(after(sums, low), (4, 8))
    high = steering(N_TM // 2, after(owners[HALF:], low), places[HALF:], offsets, gain)
    sums = after(sums, high)
    tolerance = sums[N_STN, :8]
    tolerance = tolerance + permuted(tolerance, "tm", lambda i: i ^ WINDOW)
    tolerance = tolerance[: CHAN // 128].reshape(CHAN)
    window = [sums[0]] + [
        permuted(sums[d], "stn", lambda i, d=d: (i + d) % N_STN) for d in range(1, N_STN)
    ]
    outgoing = beams(me, channels, slots, order, tolerance, window, arrived, perm, low, high)
    outgoing = outgoing.reshape(N_TM * N_STN, 1, 128)
    landed = lax.all_to_all(outgoing, ("tm", "stn"), split_axis=0, concat_axis=0, tiled=True)
    return settle(jnp.reshape(tm, (1,)).astype(jnp.int32), landed.reshape(N_TM * N_STN, 128))


def solution(mesh):
    in_specs = (P("tm", None, None, "stn", None), P(), P("tm"), P(), P(), P())
    out_specs = P("tm", None, "stn")
    return jax.shard_map(
        per_device, mesh=mesh, in_specs=in_specs, out_specs=out_specs, check_vma=False
    )
```

time: 156 us -> 134 us (0.86)
  waiting for transfers between devices: 16.7 us -> 6.43 us
  local copies, waits for them, and re-layouts: 9.33 us -> 2.35 us
  starting transfers between devices: 45.3 us -> 39.6 us
  Pallas kernels: 57.6 us -> 60.2 us
    ppermute x14, waiting for transfers between devices: 16.1 us -> 6.22 us  [permuted(): lax.ppermute(block, axis, [(i, send_to(i)) for i in range(lax.axis_size(a...]
    unnamed x28 -> x8, local copies, waits for them, and re-layouts: 7.01 us -> 0.02 us
    all_to_all x2 -> x1, starting transfers between devices: 14.5 us -> 8.33 us  [across_stations(): lax.all_to_all(blocks, 'stn', split_axis=0, concat_axis=0, tiled=True)]
    ppermute x14, starting transfers between devices: 24 us -> 26.8 us  [permuted(): lax.ppermute(block, axis, [(i, send_to(i)) for i in range(lax.axis_size(a...]
    ppermute x2 -> x1, starting transfers between devices: 6.84 us -> 4.51 us  [per_device(): received = lax.ppermute(leaving, 'tm', shift)]
    pallas_call x6 -> x5, Pallas kernels: 48.2 us -> 49.5 us  [the longest x2 31.5 us: channelize(): pl.pallas_call(functools.partial(channelize_kernel, carried), out_shape=j...]
  transfers between devices with their start and end apart: 18 -> 16, of which waited for: 7 -> 6; matrix products, arithmetic and copies ran while one was open for 3% -> 2% of each run, Pallas kernels for 25% -> 24%
where the time goes in v1:
time: 134 us; the launch traced here: 133 us
  Pallas kernels  60.2 us (45%)
  starting transfers between devices  39.6 us (30%)
  blocking collectives  23 us (17%)
  waiting for transfers between devices  6.43 us (5%)
  local copies, waits for them, and re-layouts  2.35 us (2%)
    pallas_call x2, Pallas kernels, channelize(): pl.pallas_call(functools.partial(channelize_kernel, carried), out_shape=j...  31.5 us
    ppermute x14, starting transfers between devices, permuted(): lax.ppermute(block, axis, [(i, send_to(i)) for i in range(lax.axis_size(a...  26.8 us
    all_to_all x1, blocking collectives, per_device(): lax.all_to_all(outgoing, ('tm', 'stn'), split_axis=0, concat_axis=0, tile...  23 us
    pallas_call x2, Pallas kernels, steering(): pl.pallas_call(functools.partial(steering_kernel, start), out_shape=jax.S...  15 us
    pallas_call x1, Pallas kernels, beams(): pl.pallas_call(beam_kernel, out_shape=jax.ShapeDtypeStruct((N_TM, N_STN,...  9.09 us
    all_to_all x1, starting transfers between devices, across_stations(): lax.all_to_all(blocks, 'stn', split_axis=0, concat_axis=0, tiled=True)  8.33 us
    ppermute x14, waiting for transfers between devices, permuted(): lax.ppermute(block, axis, [(i, send_to(i)) for i in range(lax.axis_size(a...  6.22 us
    ppermute x1, starting transfers between devices, per_device(): received = lax.ppermute(leaving, 'tm', shift)  4.51 us
  transfers between devices with their start and end apart: 16, of which 6 were waited for; matrix products, arithmetic and copies ran while one was open for 2% of the time, Pallas kernels for 24%

profile of v1, /device:TPU:1, one launch (start us, length us, event | category | flops | bytes accessed | tf_op | source)
XLA Modules:
  0.0 132.7 jit_solution(11658358075683388598)
XLA Ops:
  0.0 15.3 %carried.1 = bf16[8,8,96,128]{3,2,1,0:T(8,128)(2,1)S(1)} custom-call(bf16[16,2,2,32,2048]{4,3,2,1,0:T(8,128)(2,1)} %refs_3_.2, bf16[16,2,2,32,2048]{4,3,2,1,0:T(8,128)(2,1)} %refs_3_.2, bf16[16,2,2,32,2048]{4,3,2,1,0:T(8,128)(2,1)} %refs_3_.2, bf16[16,2,2,32,2048]{4,3,2,1,0:T(8,128)(2,1)} %refs_3_.2, f32[16,2048]{1,0:T(8,128)} %refs_7_.3, ...), custom_call_target="tpu_custom_call" | custom-call | flops 14000000000 | bytes 16000000 | tf_op jit(solution)/shard_map/carried/pallas_call | solution.py:197
  15.3 4.5 %collective-permute-start = (bf16[8,8,96,128]{3,2,1,0:T(8,128)(2,1)S(1)}, bf16[8,8,96,128]{3,2,1,0:T(8,128)(2,1)S(1)}, u32[]{:S(2)}, u32[]{:S(2)}) collective-permute-start(bf16[8,8,96,128]{3,2,1,0:T(8,128)(2,1)S(1)} %carried.1), channel_id=1, source_target_pairs={{0,1},{1,2},{2,3},{3,4},{4,5},{5,6},{6,7},{7,8},{8,9},{9,10},{10,1... | collective-permute-start | bytes 4718600 | tf_op jit(solution)/shard_map/ppermute | solution.py:511
  20.6 16.3 %own.1.own_ref = f32[8,8,96,128]{3,2,1,0:T(8,128)S(1)} custom-call(bf16[16,2,2,32,2048]{4,3,2,1,0:T(8,128)(2,1)} %refs_3_.2, bf16[16,2,2,32,2048]{4,3,2,1,0:T(8,128)(2,1)} %refs_3_.2, bf16[16,2,2,32,2048]{4,3,2,1,0:T(8,128)(2,1)} %refs_3_.2, bf16[16,2,2,32,2048]{4,3,2,1,0:T(8,128)(2,1)} %refs_3_.2, f32[16,2048]{1,0:T(8,128)} %refs_7_.3, f32[16,2048]{1,0:T(8,128)} %refs_7_.3, ...), custom_call_target="tpu_custom_call" | custom-call | flops 14000000000 | bytes 16000000 | tf_op jit(solution)/shard_map/own/pallas_call | solution.py:197
  37.1 2.9 %combine.1 = (bf16[8,8,96,128]{3,2,1,0:T(8,128)(2,1)}, f32[9,48,128]{2,1,0:T(8,128)S(1)}) custom-call(s32[1]{0:T(128)} %bitcast.1.me_ref, f32[8,8,96,128]{3,2,1,0:T(8,128)S(1)} %own.1.own_ref, bf16[8,8,96,128]{3,2,1,0:T(8,128)(2,1)S(1)} %collective-permute-done.received_ref, f32[48,128]{1,0:T(8,128)S(1)} %pad.4.tol_ref), custom_call_target="tpu_custom_call" | custom-call | flops 8000000 | bytes 8000000 | tf_op jit(solution)/shard_map/combine/pallas_call | solution.py:246
  40.1 8.3 %all-to-all-start = ((bf16[8,8,96,128]{3,2,1,0:T(8,128)(2,1)}), bf16[8,8,96,128]{3,2,1,0:T(8,128)(2,1)S(1)}, u32[]{:S(2)}, u32[]{:S(2)}) async-start(bf16[8,8,96,128]{3,2,1,0:T(8,128)(2,1)} %get-tuple-element.14), calls=%async_computation | async-start | bytes 3145728 | tf_op jit(solution)/shard_map/all_to_all | solution.py:478
  49.1 0.8 multiply_add_fusion.offset_ref
  50.0 2.8 %collective-permute-start.3 = (f32[9,48,128]{2,1,0:T(8,128)S(1)}, f32[9,48,128]{2,1,0:T(8,128)S(1)}, u32[]{:S(2)}, u32[]{:S(2)}) collective-permute-start(f32[9,48,128]{2,1,0:T(8,128)S(1)} %get-tuple-element.13), channel_id=1, source_target_pairs={{0,3},{1,2},{2,1},{3,0},{4,7},{5,6},{6,5},{7,4},{8,11},{9,10},{10,... | collective-permute-start | bytes 663560 | tf_op jit(solution)/shard_map/ppermute | solution.py:486
  53.2 0.8 broadcast_in_dim.11.gain_ref
  54.0 7.4 %steering.2.refs_10_ = bf16[24,256,512]{2,1,0:T(8,128)(2,1)} custom-call(s32[24]{0:T(128)} %get-tuple-element.15.t_ref, s32[24]{0:T(128)} %get-tuple-element.29.o_ref, s32[256,256]{1,0:T(8,128)} %multiply_add_fusion.offset_ref, f32[256,256]{1,0:T(8,128)} %broadcast_in_dim.11.gain_ref), custom_call_target="tpu_custom_call" | custom-call | flops 40000 | bytes 12600 | tf_op jit(solution)/shard_map/steering/pallas_call | solution.py:326
  61.8 5.6 %collective-permute-start.6 = (f32[9,48,128]{2,1,0:T(8,128)S(1)}, f32[9,48,128]{2,1,0:T(8,128)S(1)}, u32[]{:S(2)}, u32[]{:S(2)}) collective-permute-start(f32[9,48,128]{2,1,0:T(8,128)S(1)} %add_add_fusion.1), channel_id=1, source_target_pairs={{0,12},{1,13},{2,14},{3,15},{4,8},{5,9},{6,10},{7,11},{8,4},{9,5},... | collective-permute-start | bytes 663560 | tf_op jit(solution)/shard_map/ppermute | solution.py:486
  67.9 7.6 %steering.3.refs_11_ = bf16[24,256,512]{2,1,0:T(8,128)(2,1)} custom-call(s32[24]{0:T(128)} %get-tuple-element.17.t_ref, s32[24]{0:T(128)} %get-tuple-element.27.o_ref, s32[256,256]{1,0:T(8,128)} %multiply_add_fusion.offset_ref, f32[256,256]{1,0:T(8,128)} %broadcast_in_dim.11.gain_ref), custom_call_target="tpu_custom_call" | custom-call | flops 40000 | bytes 12600 | tf_op jit(solution)/shard_map/steering/pallas_call | solution.py:326
  75.6 2.5 %collective-permute-done.5 = f32[9,48,128]{2,1,0:T(8,128)S(1)} collective-permute-done((f32[9,48,128]{2,1,0:T(8,128)S(1)}, f32[9,48,128]{2,1,0:T(8,128)S(1)}, u32[]{:S(2)}, u32[]{:S(2)}) %collective-permute-start.5) | collective-permute-done | bytes 221216 | tf_op jit(solution)/shard_map/ppermute | solution.py:486
  78.2 3.5 %collective-permute-start.7 = (f32[8,128]{1,0:T(8,128)S(1)}, f32[8,128]{1,0:T(8,128)S(1)}, u32[]{:S(2)}, u32[]{:S(2)}) collective-permute-start(f32[8,128]{1,0:T(8,128)S(1)} %slice_bitcast_fusion.8), channel_id=1, source_target_pairs={{0,16},{1,17},{2,18},{3,19},{4,20},{5,21},{6,22},{7,23},{8,24},{9,... | collective-permute-start | bytes 12296 | tf_op jit(solution)/shard_map/ppermute | solution.py:486
  81.7 3.0 %collective-permute-start.14 = (f32[48,128]{1,0:T(8,128)S(1)}, f32[48,128]{1,0:T(8,128)S(1)}, u32[]{:S(2)}, u32[]{:S(2)}) collective-permute-start(f32[48,128]{1,0:T(8,128)S(1)} %get-tuple-element.19), channel_id=1, source_target_pairs={{0,224},{32,0},{64,32},{96,64},{128,96},{160,128},{192,160},{224,1... | collective-permute-start | bytes 73736 | tf_op jit(solution)/shard_map/ppermute | solution.py:486
  84.7 2.1 %collective-permute-start.13 = (f32[48,128]{1,0:T(8,128)S(1)}, f32[48,128]{1,0:T(8,128)S(1)}, u32[]{:S(2)}, u32[]{:S(2)}) collective-permute-start(f32[48,128]{1,0:T(8,128)S(1)} %get-tuple-element.20), channel_id=1, source_target_pairs={{0,192},{32,224},{64,0},{96,32},{128,64},{160,96},{192,128},{224,1... | collective-permute-start | bytes 73736 | tf_op jit(solution)/shard_map/ppermute | solution.py:486
  86.8 1.2 collective-permute-start.12
  88.0 3.3 %collective-permute-start.11 = (f32[48,128]{1,0:T(8,128)S(1)}, f32[48,128]{1,0:T(8,128)S(1)}, u32[]{:S(2)}, u32[]{:S(2)}) collective-permute-start(f32[48,128]{1,0:T(8,128)S(1)} %get-tuple-element.22), channel_id=1, source_target_pairs={{0,128},{32,160},{64,192},{96,224},{128,0},{160,32},{192,64},{224,... | collective-permute-start | bytes 73736 | tf_op jit(solution)/shard_map/ppermute | solution.py:486
  91.3 3.2 %collective-permute-start.9 = (f32[48,128]{1,0:T(8,128)S(1)}, f32[48,128]{1,0:T(8,128)S(1)}, u32[]{:S(2)}, u32[]{:S(2)}) collective-permute-start(f32[48,128]{1,0:T(8,128)S(1)} %get-tuple-element.24), channel_id=1, source_target_pairs={{0,64},{32,96},{64,128},{96,160},{128,192},{160,224},{192,0},{224,... | collective-permute-start | bytes 73736 | tf_op jit(solution)/shard_map/ppermute | solution.py:486
  94.6 1.2 collective-permute-start.8
  95.8 1.5 %collective-permute-done.10.refs_3_ = f32[48,128]{1,0:T(8,128)S(1)} collective-permute-done((f32[48,128]{1,0:T(8,128)S(1)}, f32[48,128]{1,0:T(8,128)S(1)}, u32[]{:S(2)}, u32[]{:S(2)}) %collective-permute-start.10) | collective-permute-done | bytes 24608 | tf_op jit(solution)/shard_map/ppermute | solution.py:486
  97.3 1.7 %collective-permute-done.8.refs_1_ = f32[48,128]{1,0:T(8,128)S(1)} collective-permute-done((f32[48,128]{1,0:T(8,128)S(1)}, f32[48,128]{1,0:T(8,128)S(1)}, u32[]{:S(2)}, u32[]{:S(2)}) %collective-permute-start.8) | collective-permute-done | bytes 24608 | tf_op jit(solution)/shard_map/ppermute | solution.py:486
  99.0 9.1 %beams.1 = f32[32,8,128]{2,1,0:T(8,128)S(1)} custom-call(s32[1]{0:T(128)} %bitcast.1.me_ref, s32[48]{0:T(128)S(1)} %get-tuple-element.33.chan_ref, s32[48]{0:T(128)S(1)} %get-tuple-element.32.slot_ref, s32[48]{0:T(128)S(1)} %get-tuple-element.31.order_ref, f32[384]{0:T(512)S(1)} %slice_bitcast_fusion.9.tol_ref, f32[48,128]{1,0:T(8,128)S(1)} %get-tuple-element.26.refs_0_, ...), custom_call_target="tpu_custom_call" | custom-call | flops 2400000000 | bytes 16000000 | tf_op jit(solution)/shard_map/beams/pallas_call | solution.py:436
  108.1 23.0 %all_to_all.10 = f32[256,1,128]{2,1,0:T(1,128)} all-to-all(f32[256,1,128]{2,1,0:T(1,128)S(1)} %bitcast.46), channel_id=1, replica_groups=mesh['stn'=8,'tm'=32] {'tm','stn'}, dimensions={0} | all-to-all | bytes 262144 | tf_op jit(solution)/shard_map/all_to_all | solution.py:532
  131.1 1.7 %settle.1 = f32[12,32,32]{2,1,0:T(8,128)} custom-call(s32[1]{0:T(128)} %bitcast.t_ref, f32[256,128]{1,0:T(8,128)} %bitcast.47), custom_call_target="tpu_custom_call" | custom-call | tf_op jit(solution)/shard_map/settle/pallas_call | solution.py:468
  (42 shorter events, 3.4 us)
Async XLA Ops:
  0.0 19.8 %copy-start.3 = (f32[12]{0:T(128)S(1)}, f32[12]{0:T(128)}, u32[]{:S(2)}) copy-start(f32[12]{0:T(128)} %param.11) | copy-start | bytes 148
  15.3 21.9 %collective-permute-start = (bf16[8,8,96,128]{3,2,1,0:T(8,128)(2,1)S(1)}, bf16[8,8,96,128]{3,2,1,0:T(8,128)(2,1)S(1)}, u32[]{:S(2)}, u32[]{:S(2)}) collective-permute-start(bf16[8,8,96,128]{3,2,1,0:T(8,128)(2,1)S(1)} %carried.1), channel_id=1, source_target_pairs={{0,1},{1,2},{2,3},{3,4},{4,5},{5,6},{6,7},{7,8},{8,9},{9,10},{10,1... | collective-permute-start | bytes 4718600 | tf_op jit(solution)/shard_map/ppermute | solution.py:511
  40.1 8.4 %copy-start = (s32[256,2]{0,1:T(2,128)S(1)}, s32[256,2]{0,1:T(2,128)}, u32[]{:S(2)}) copy-start(s32[256,2]{0,1:T(2,128)} %param.12) | copy-start | bytes 6148
  40.1 8.4 %copy-start.1 = (s32[256,2]{0,1:T(2,128)S(1)}, s32[256,2]{0,1:T(2,128)}, u32[]{:S(2)}) copy-start(s32[256,2]{0,1:T(2,128)} %param.13) | copy-start | bytes 6148
  40.1 13.1 %copy-start.2 = (s32[256]{0:T(256)S(1)}, s32[256]{0:T(256)}, u32[]{:S(2)}) copy-start(s32[256]{0:T(256)} %param.14) | copy-start | bytes 3076
  40.1 58.9 %all-to-all-start = ((bf16[8,8,96,128]{3,2,1,0:T(8,128)(2,1)}), bf16[8,8,96,128]{3,2,1,0:T(8,128)(2,1)S(1)}, u32[]{:S(2)}, u32[]{:S(2)}) async-start(bf16[8,8,96,128]{3,2,1,0:T(8,128)(2,1)} %get-tuple-element.14), calls=%async_computation | async-start | bytes 3145728 | tf_op jit(solution)/shard_map/all_to_all | solution.py:478
  50.0 11.4 %collective-permute-start.3 = (f32[9,48,128]{2,1,0:T(8,128)S(1)}, f32[9,48,128]{2,1,0:T(8,128)S(1)}, u32[]{:S(2)}, u32[]{:S(2)}) collective-permute-start(f32[9,48,128]{2,1,0:T(8,128)S(1)} %get-tuple-element.13), channel_id=1, source_target_pairs={{0,3},{1,2},{2,1},{3,0},{4,7},{5,6},{6,5},{7,4},{8,11},{9,10},{10,... | collective-permute-start | bytes 663560 | tf_op jit(solution)/shard_map/ppermute | solution.py:486
  52.7 9.0 %collective-permute-start.2 = (f32[9,48,128]{2,1,0:T(8,128)S(1)}, f32[9,48,128]{2,1,0:T(8,128)S(1)}, u32[]{:S(2)}, u32[]{:S(2)}) collective-permute-start(f32[9,48,128]{2,1,0:T(8,128)S(1)} %get-tuple-element.13), channel_id=1, source_target_pairs={{0,2},{1,3},{2,0},{3,1},{4,6},{5,7},{6,4},{7,5},{8,10},{9,11},{10,... | collective-permute-start | bytes 663560 | tf_op jit(solution)/shard_map/ppermute | solution.py:486
  52.7 9.0 %collective-permute-start.1 = (f32[9,48,128]{2,1,0:T(8,128)S(1)}, f32[9,48,128]{2,1,0:T(8,128)S(1)}, u32[]{:S(2)}, u32[]{:S(2)}) collective-permute-start(f32[9,48,128]{2,1,0:T(8,128)S(1)} %get-tuple-element.13), channel_id=1, source_target_pairs={{0,1},{1,0},{2,3},{3,2},{4,5},{5,4},{6,7},{7,6},{8,9},{9,8},{10,11... | collective-permute-start | bytes 663560 | tf_op jit(solution)/shard_map/ppermute | solution.py:486
  61.8 13.7 %collective-permute-start.6 = (f32[9,48,128]{2,1,0:T(8,128)S(1)}, f32[9,48,128]{2,1,0:T(8,128)S(1)}, u32[]{:S(2)}, u32[]{:S(2)}) collective-permute-start(f32[9,48,128]{2,1,0:T(8,128)S(1)} %add_add_fusion.1), channel_id=1, source_target_pairs={{0,12},{1,13},{2,14},{3,15},{4,8},{5,9},{6,10},{7,11},{8,4},{9,5},... | collective-permute-start | bytes 663560 | tf_op jit(solution)/shard_map/ppermute | solution.py:486
  67.4 10.6 %collective-permute-start.5 = (f32[9,48,128]{2,1,0:T(8,128)S(1)}, f32[9,48,128]{2,1,0:T(8,128)S(1)}, u32[]{:S(2)}, u32[]{:S(2)}) collective-permute-start(f32[9,48,128]{2,1,0:T(8,128)S(1)} %add_add_fusion.1), channel_id=1, source_target_pairs={{0,8},{1,9},{2,10},{3,11},{4,12},{5,13},{6,14},{7,15},{8,0},{9,1},... | collective-permute-start | bytes 663560 | tf_op jit(solution)/shard_map/ppermute | solution.py:486
  67.6 10.6 %collective-permute-start.4 = (f32[9,48,128]{2,1,0:T(8,128)S(1)}, f32[9,48,128]{2,1,0:T(8,128)S(1)}, u32[]{:S(2)}, u32[]{:S(2)}) collective-permute-start(f32[9,48,128]{2,1,0:T(8,128)S(1)} %add_add_fusion.1), channel_id=1, source_target_pairs={{0,4},{1,5},{2,6},{3,7},{4,0},{5,1},{6,2},{7,3},{8,12},{9,13},{10,... | collective-permute-start | bytes 663560 | tf_op jit(solution)/shard_map/ppermute | solution.py:486
  78.2 13.1 %collective-permute-start.7 = (f32[8,128]{1,0:T(8,128)S(1)}, f32[8,128]{1,0:T(8,128)S(1)}, u32[]{:S(2)}, u32[]{:S(2)}) collective-permute-start(f32[8,128]{1,0:T(8,128)S(1)} %slice_bitcast_fusion.8), channel_id=1, source_target_pairs={{0,16},{1,17},{2,18},{3,19},{4,20},{5,21},{6,22},{7,23},{8,24},{9,... | collective-permute-start | bytes 12296 | tf_op jit(solution)/shard_map/ppermute | solution.py:486
  81.7 9.6 %collective-permute-start.14 = (f32[48,128]{1,0:T(8,128)S(1)}, f32[48,128]{1,0:T(8,128)S(1)}, u32[]{:S(2)}, u32[]{:S(2)}) collective-permute-start(f32[48,128]{1,0:T(8,128)S(1)} %get-tuple-element.19), channel_id=1, source_target_pairs={{0,224},{32,0},{64,32},{96,64},{128,96},{160,128},{192,160},{224,1... | collective-permute-start | bytes 73736 | tf_op jit(solution)/shard_map/ppermute | solution.py:486
  84.7 9.8 %collective-permute-start.13 = (f32[48,128]{1,0:T(8,128)S(1)}, f32[48,128]{1,0:T(8,128)S(1)}, u32[]{:S(2)}, u32[]{:S(2)}) collective-permute-start(f32[48,128]{1,0:T(8,128)S(1)} %get-tuple-element.20), channel_id=1, source_target_pairs={{0,192},{32,224},{64,0},{96,32},{128,64},{160,96},{192,128},{224,1... | collective-permute-start | bytes 73736 | tf_op jit(solution)/shard_map/ppermute | solution.py:486
  86.8 8.9 %collective-permute-start.12 = (f32[48,128]{1,0:T(8,128)S(1)}, f32[48,128]{1,0:T(8,128)S(1)}, u32[]{:S(2)}, u32[]{:S(2)}) collective-permute-start(f32[48,128]{1,0:T(8,128)S(1)} %get-tuple-element.21), channel_id=1, source_target_pairs={{0,160},{32,192},{64,224},{96,0},{128,32},{160,64},{192,96},{224,1... | collective-permute-start | bytes 73736 | tf_op jit(solution)/shard_map/ppermute | solution.py:486
  88.0 7.8 %collective-permute-start.11 = (f32[48,128]{1,0:T(8,128)S(1)}, f32[48,128]{1,0:T(8,128)S(1)}, u32[]{:S(2)}, u32[]{:S(2)}) collective-permute-start(f32[48,128]{1,0:T(8,128)S(1)} %get-tuple-element.22), channel_id=1, source_target_pairs={{0,128},{32,160},{64,192},{96,224},{128,0},{160,32},{192,64},{224,... | collective-permute-start | bytes 73736 | tf_op jit(solution)/shard_map/ppermute | solution.py:486
  91.3 6.0 %collective-permute-start.10 = (f32[48,128]{1,0:T(8,128)S(1)}, f32[48,128]{1,0:T(8,128)S(1)}, u32[]{:S(2)}, u32[]{:S(2)}) collective-permute-start(f32[48,128]{1,0:T(8,128)S(1)} %get-tuple-element.23), channel_id=1, source_target_pairs={{0,96},{32,128},{64,160},{96,192},{128,224},{160,0},{192,32},{224,... | collective-permute-start | bytes 73736 | tf_op jit(solution)/shard_map/ppermute | solution.py:486
  91.3 6.0 %collective-permute-start.9 = (f32[48,128]{1,0:T(8,128)S(1)}, f32[48,128]{1,0:T(8,128)S(1)}, u32[]{:S(2)}, u32[]{:S(2)}) collective-permute-start(f32[48,128]{1,0:T(8,128)S(1)} %get-tuple-element.24), channel_id=1, source_target_pairs={{0,64},{32,96},{64,128},{96,160},{128,192},{160,224},{192,0},{224,... | collective-permute-start | bytes 73736 | tf_op jit(solution)/shard_map/ppermute | solution.py:486
  94.6 4.4 %collective-permute-start.8 = (f32[48,128]{1,0:T(8,128)S(1)}, f32[48,128]{1,0:T(8,128)S(1)}, u32[]{:S(2)}, u32[]{:S(2)}) collective-permute-start(f32[48,128]{1,0:T(8,128)S(1)} %get-tuple-element.25), channel_id=1, source_target_pairs={{0,32},{32,64},{64,96},{96,128},{128,160},{160,192},{192,224},{224... | collective-permute-start | bytes 73736 | tf_op jit(solution)/shard_map/ppermute | solution.py:486

commit v2 on v1

--- a/solution.py
+++ b/solution.py
@@ -258,7 +258,7 @@
     )(me, own, received, tolerances)
 
 
-STATION_ROWS = 32
+STATION_ROWS = 64
 
 
 def turn(offsets, number):
@@ -283,8 +283,18 @@
     return a[0] * b[0] - a[1] * b[1], a[0] * b[1] + a[1] * b[0]
 
 
-def steering_kernel(start, t_ref, o_ref, offset_ref, gain_ref, out_ref, coarse, fine):
-    offsets = offset_ref[...]
+def steering_kernel(start, me_ref, plan_ref, coords_ref, flags_ref, pointings_ref, out_ref, coarse, fine):
+    me = me_ref[0]
+    shape = (STATION_ROWS, STATIONS)
+    station = pl.program_id(0) * STATION_ROWS + lax.broadcasted_iota(jnp.int32, shape, 0)
+    mine = station == lax.broadcasted_iota(jnp.int32, shape, 1)
+
+    def column(row):
+        return jnp.sum(jnp.where(mine, row.astype(F32), 0.0), 1, keepdims=True)
+
+    east = column(coords_ref[0:1, :]).astype(jnp.int32)
+    north = column(coords_ref[1:2, :]).astype(jnp.int32)
+    offsets = east * pointings_ref[0:1, :] + north * pointings_ref[1:2, :]
     single = turn(offsets, 1)
     pair = times(single, single)
     fine[0, 0], fine[0, 1] = single
@@ -294,7 +304,8 @@
     stride = (fine[OWNED - 1, 0], fine[OWNED - 1, 1])
     double = times(stride, stride)
     fast = times(double, double)
-    gain = gain_ref[...]
+    gain = column((1 - flags_ref[...]).astype(F32) * (1.0 / math.sqrt(STATIONS)))
+    gain = jnp.broadcast_to(gain, (STATION_ROWS, BEAMS))
     value = (gain, jnp.zeros_like(gain))
     if start:
         value = tuple(part * gain for part in turn(offsets, OWNED * start))
@@ -308,7 +319,8 @@
     def channels(n, _):
         for i in range(4):
             at = 4 * n + i
-            t, o = t_ref[at] - start, o_ref[at]
+            c = at + (start and HALF)
+            t, o = plan_ref[me, 3 * LOCAL_CHAN + c] - start, plan_ref[me, 4 * LOCAL_CHAN + c]
             real, imag = times((coarse[t, 0], coarse[t, 1]), (fine[o, 0], fine[o, 1]))
             out_ref[at, :, :BEAMS] = real.astype(BF16)
             out_ref[at, :, BEAMS:] = imag.astype(BF16)
@@ -320,14 +332,14 @@
 HALF = LOCAL_CHAN // 2
 
 
-def steering(start, owners, places, offsets, gain):
+def steering(start, me, plans, coords, flags, pointings):
     smem = pl.BlockSpec(memory_space=pltpu.SMEM)
-    rows = pl.BlockSpec((STATION_ROWS, BEAMS), lambda i: (i, 0))
+    vmem = pl.BlockSpec(memory_space=pltpu.VMEM)
     return pl.pallas_call(
         functools.partial(steering_kernel, start),
         out_shape=jax.ShapeDtypeStruct((HALF, STATIONS, 2 * BEAMS), BF16),
         grid=(STATIONS // STATION_ROWS,),
-        in_specs=[smem, smem, rows, rows],
+        in_specs=[smem, smem, vmem, vmem, vmem],
         out_specs=pl.BlockSpec((HALF, STATION_ROWS, 2 * BEAMS), lambda i: (0, i, 0)),
         scratch_shapes=[
             pltpu.VMEM((N_TM // 2, 2, STATION_ROWS, BEAMS), F32),
@@ -338,7 +350,7 @@
         ),
         cost_estimate=pl.CostEstimate(flops=40_000, bytes_accessed=12_600, transcendentals=0),
         name="steering",
-    )(owners, places, offsets, gain)
+    )(me, plans, coords, flags, pointings)
 
 
 def place_stations(in_ref, polar, perm_ref, out_ref):
@@ -361,7 +373,7 @@
 CHUNKS = LOCAL_CHAN // BLOCK
 
 
-def beam_kernel(me_ref, chan_ref, slot_ref, order_ref, tol_ref, *refs):
+def beam_kernel(me_ref, plan_ref, tol_ref, *refs):
     sum_refs = refs[:N_STN]
     in_ref, perm_ref, low_ref, high_ref, out_ref = refs[N_STN : N_STN + 5]
     window_sums, ordered, first_placed, second_placed, perm, weights, powers, arrival = refs[N_STN + 5 :]
@@ -402,8 +414,8 @@
         load(chunk).wait()
         for inner in range(BLOCK):
             visit = chunk * BLOCK + inner
-            local = order_ref[visit]
-            tolerance = tol_ref[chan_ref[visit]]
+            local = plan_ref[me_ref[0], 2 * LOCAL_CHAN + visit]
+            tolerance = tol_ref[plan_ref[me_ref[0], visit]]
             rows = []
             for polar, ref in enumerate((first_placed, second_placed)):
                 s1 = window_sums[polar, 0, pl.ds(local, 1), :]
@@ -419,7 +431,7 @@
             real = product[:32, :BEAMS] - product[32:, BEAMS:]
             imag = product[:32, BEAMS:] + product[32:, :BEAMS]
             power = jnp.sum(real * real + imag * imag, 0, keepdims=True) * (1.0 / (2.0 * INTEG))
-            powers[pl.ds(slot_ref[visit], 1), :] = power
+            powers[pl.ds(plan_ref[me_ref[0], LOCAL_CHAN + visit], 1), :] = power
 
     share = BEAMS // N_STN
     out_ref[...] = jnp.zeros_like(out_ref)
@@ -429,14 +441,14 @@
             out_ref[:, j, slot * share : (slot + 1) * share] = rows[:, j * share : (j + 1) * share]
 
 
-def beams(me, channels, slots, order, tolerance, sums, arrived, perm, low, high):
+def beams(me, plans, tolerance, sums, arrived, perm, low, high):
     smem = pl.BlockSpec(memory_space=pltpu.SMEM)
     vmem = pl.BlockSpec(memory_space=pltpu.VMEM)
     low, high, perm = (pltpu.with_memory_space_constraint(x, pltpu.HBM) for x in (low, high, perm))
     return pl.pallas_call(
         beam_kernel,
         out_shape=jax.ShapeDtypeStruct((N_TM, N_STN, 128), F32),
-        in_specs=[smem] * 5 + [vmem] * (N_STN + 1) + [pl.BlockSpec(memory_space=pl.ANY)] * 3,
+        in_specs=[smem] * 3 + [vmem] * (N_STN + 1) + [pl.BlockSpec(memory_space=pl.ANY)] * 3,
         out_specs=vmem,
         scratch_shapes=[
             pltpu.VMEM((2, 2, LOCAL_CHAN, STATIONS), F32),
@@ -451,7 +463,7 @@
         compiler_params=pltpu.CompilerParams(vmem_limit_bytes=36 * 1024 * 1024),
         cost_estimate=pl.CostEstimate(flops=2_400_000_000, bytes_accessed=16_000_000, transcendentals=0),
         name="beams",
-    )(me, channels, slots, order, tolerance, *sums, arrived, perm, low, high)
+    )(me, plans, tolerance, *sums, arrived, perm, low, high)
 
 
 def settle_kernel(t_ref, in_ref, out_ref):
@@ -501,11 +513,8 @@
 
     visited = np.array(VISITED)
     plans = np.stack([visited, np.array(VISITED_SLOTS), np.array(ORDER), visited // OWNED, visited % OWNED], 1)
-    plan = lax.dynamic_index_in_dim(jnp.asarray(plans.astype(np.int32)), stn, 0, False)
-    channels, slots, order, owners, places = plan
-    offsets = station_coords[:, 0:1] * pointings[None, :, 0] + station_coords[:, 1:2] * pointings[None, :, 1]
-    live = (1 - station_flags).astype(F32) * (1.0 / math.sqrt(STATIONS))
-    gain = jnp.broadcast_to(live[:, None], (STATIONS, BEAMS))
+    plans = jnp.asarray(plans.astype(np.int32).reshape(N_STN, 5 * LOCAL_CHAN))
+    geometry = (station_coords.T, station_flags[None, :], pointings.T)
 
     leaving = channelize(voltages, taps, table, True)
     received = lax.ppermute(leaving, "tm", shift)
@@ -517,9 +526,9 @@
     blocks, sums = combine(me, own, received, tolerances)
     arrived = across_stations(blocks)
     sums = window_round(sums, (1, 2))
-    low = steering(0, after(owners[:HALF], blocks), places[:HALF], offsets, gain)
+    low = steering(0, after(me, blocks), plans, *geometry)
     sums = window_round(after(sums, low), (4, 8))
-    high = steering(N_TM // 2, after(owners[HALF:], low), places[HALF:], offsets, gain)
+    high = steering(N_TM // 2, after(me, low), plans, *geometry)
     sums = after(sums, high)
     tolerance = sums[N_STN, :8]
     tolerance = tolerance + permuted(tolerance, "tm", lambda i: i ^ WINDOW)
@@ -527,7 +536,7 @@
     window = [sums[0]] + [
         permuted(sums[d], "stn", lambda i, d=d: (i + d) % N_STN) for d in range(1, N_STN)
     ]
-    outgoing = beams(me, channels, slots, order, tolerance, window, arrived, perm, low, high)
+    outgoing = beams(me, plans, tolerance, window, arrived, perm, low, high)
     outgoing = outgoing.reshape(N_TM * N_STN, 1, 128)
     landed = lax.all_to_all(outgoing, ("tm", "stn"), split_axis=0, concat_axis=0, tiled=True)
     return settle(jnp.reshape(tm, (1,)).astype(jnp.int32), landed.reshape(N_TM * N_STN, 128))

time: 134 us -> 131 us (0.978)
  waiting for transfers between devices: 6.43 us -> 8.89 us
  local copies, waits for them, and re-layouts: 2.35 us -> 0.14 us
    ppermute x14, waiting for transfers between devices: 6.22 us -> 8.02 us  [permuted(): lax.ppermute(block, axis, [(i, send_to(i)) for i in range(lax.axis_size(a...]
  transfers between devices with their start and end apart: 16 -> 16, of which waited for: 6 -> 6; matrix products, arithmetic and copies ran while one was open for 2% -> 0% of each run, Pallas kernels for 24% -> 23%
where the time goes in v2:
time: 131 us
  Pallas kernels  59.5 us (45%)
  starting transfers between devices  39 us (30%)
  blocking collectives  23.1 us (18%)
  waiting for transfers between devices  8.89 us (7%)
    pallas_call x2, Pallas kernels, channelize(): pl.pallas_call(functools.partial(channelize_kernel, carried), out_shape=j...  31.5 us
    ppermute x14, starting transfers between devices, permuted(): lax.ppermute(block, axis, [(i, send_to(i)) for i in range(lax.axis_size(a...  26.3 us
    all_to_all x1, blocking collectives, per_device(): lax.all_to_all(outgoing, ('tm', 'stn'), split_axis=0, concat_axis=0, tile...  23.1 us
    pallas_call x2, Pallas kernels, steering(): pl.pallas_call(functools.partial(steering_kernel, start), out_shape=jax.S...  14.1 us
    pallas_call x1, Pallas kernels, beams(): pl.pallas_call(beam_kernel, out_shape=jax.ShapeDtypeStruct((N_TM, N_STN,...  9.19 us
    all_to_all x1, starting transfers between devices, across_stations(): lax.all_to_all(blocks, 'stn', split_axis=0, concat_axis=0, tiled=True)  8.2 us
    ppermute x14, waiting for transfers between devices, permuted(): lax.ppermute(block, axis, [(i, send_to(i)) for i in range(lax.axis_size(a...  8.02 us
    ppermute x1, starting transfers between devices, per_device(): received = lax.ppermute(leaving, 'tm', shift)  4.51 us
  transfers between devices with their start and end apart: 16, of which 6 were waited for; matrix products, arithmetic and copies ran while one was open for 0% of the time, Pallas kernels for 23%

profile of v2, /device:TPU:1, one launch (start us, length us, event | category | flops | bytes accessed | tf_op | source)
XLA Modules:
  0.0 131.0 jit_solution(16276424538998051310)
XLA Ops:
  0.0 15.3 %carried.1 = bf16[8,8,96,128]{3,2,1,0:T(8,128)(2,1)S(1)} custom-call(bf16[16,2,2,32,2048]{4,3,2,1,0:T(8,128)(2,1)} %refs_3_.2, bf16[16,2,2,32,2048]{4,3,2,1,0:T(8,128)(2,1)} %refs_3_.2, bf16[16,2,2,32,2048]{4,3,2,1,0:T(8,128)(2,1)} %refs_3_.2, bf16[16,2,2,32,2048]{4,3,2,1,0:T(8,128)(2,1)} %refs_3_.2, f32[16,2048]{1,0:T(8,128)} %refs_7_.3, ...), custom_call_target="tpu_custom_call" | custom-call | flops 14000000000 | bytes 16000000 | tf_op jit(solution)/shard_map/carried/pallas_call | solution.py:197
  15.3 4.5 %collective-permute-start = (bf16[8,8,96,128]{3,2,1,0:T(8,128)(2,1)S(1)}, bf16[8,8,96,128]{3,2,1,0:T(8,128)(2,1)S(1)}, u32[]{:S(2)}, u32[]{:S(2)}) collective-permute-start(bf16[8,8,96,128]{3,2,1,0:T(8,128)(2,1)S(1)} %carried.1), channel_id=1, source_target_pairs={{0,1},{1,2},{2,3},{3,4},{4,5},{5,6},{6,7},{7,8},{8,9},{9,10},{10,1... | collective-permute-start | bytes 4718600 | tf_op jit(solution)/shard_map/ppermute | solution.py:520
  19.9 16.3 %own.1.own_ref = f32[8,8,96,128]{3,2,1,0:T(8,128)S(1)} custom-call(bf16[16,2,2,32,2048]{4,3,2,1,0:T(8,128)(2,1)} %refs_3_.2, bf16[16,2,2,32,2048]{4,3,2,1,0:T(8,128)(2,1)} %refs_3_.2, bf16[16,2,2,32,2048]{4,3,2,1,0:T(8,128)(2,1)} %refs_3_.2, bf16[16,2,2,32,2048]{4,3,2,1,0:T(8,128)(2,1)} %refs_3_.2, f32[16,2048]{1,0:T(8,128)} %refs_7_.3, f32[16,2048]{1,0:T(8,128)} %refs_7_.3, ...), custom_call_target="tpu_custom_call" | custom-call | flops 14000000000 | bytes 16000000 | tf_op jit(solution)/shard_map/own/pallas_call | solution.py:197
  36.2 0.9 collective-permute-done.received_ref
  37.1 2.9 %combine.1 = (bf16[8,8,96,128]{3,2,1,0:T(8,128)(2,1)}, f32[9,48,128]{2,1,0:T(8,128)S(1)}) custom-call(s32[1]{0:T(128)} %bitcast.1.me_ref, f32[8,8,96,128]{3,2,1,0:T(8,128)S(1)} %own.1.own_ref, bf16[8,8,96,128]{3,2,1,0:T(8,128)(2,1)S(1)} %collective-permute-done.received_ref, f32[48,128]{1,0:T(8,128)S(1)} %pad.4.tol_ref), custom_call_target="tpu_custom_call" | custom-call | flops 8000000 | bytes 8000000 | tf_op jit(solution)/shard_map/combine/pallas_call | solution.py:246
  40.1 8.2 %all-to-all-start = ((bf16[8,8,96,128]{3,2,1,0:T(8,128)(2,1)}), bf16[8,8,96,128]{3,2,1,0:T(8,128)(2,1)S(1)}, u32[]{:S(2)}, u32[]{:S(2)}) async-start(bf16[8,8,96,128]{3,2,1,0:T(8,128)(2,1)} %get-tuple-element.14), calls=%async_computation | async-start | bytes 3145728 | tf_op jit(solution)/shard_map/all_to_all | solution.py:490
  48.3 2.8 %collective-permute-start.3 = (f32[9,48,128]{2,1,0:T(8,128)S(1)}, f32[9,48,128]{2,1,0:T(8,128)S(1)}, u32[]{:S(2)}, u32[]{:S(2)}) collective-permute-start(f32[9,48,128]{2,1,0:T(8,128)S(1)} %get-tuple-element.13), channel_id=1, source_target_pairs={{0,3},{1,2},{2,1},{3,0},{4,7},{5,6},{6,5},{7,4},{8,11},{9,10},{10,... | collective-permute-start | bytes 663560 | tf_op jit(solution)/shard_map/ppermute | solution.py:498
  51.5 6.9 %steering.2.refs_10_ = bf16[24,256,512]{2,1,0:T(8,128)(2,1)} custom-call(s32[1]{0:T(128)} %bitcast.1.me_ref, s32[8,240]{1,0:T(8,128)} %constant.36.clone.plan_ref, s32[2,256]{1,0:T(2,128)} %bitcast.33, s32[1,256]{1,0:T(1,128)} %bitcast.37, s32[2,256]{1,0:T(2,128)} %bitcast.35), custom_call_target="tpu_custom_call" | custom-call | flops 40000 | bytes 12600 | tf_op jit(solution)/shard_map/steering/pallas_call | solution.py:338
  58.4 1.6 %collective-permute-done.2 = f32[9,48,128]{2,1,0:T(8,128)S(1)} collective-permute-done((f32[9,48,128]{2,1,0:T(8,128)S(1)}, f32[9,48,128]{2,1,0:T(8,128)S(1)}, u32[]{:S(2)}, u32[]{:S(2)}) %collective-permute-start.2) | collective-permute-done | bytes 221216 | tf_op jit(solution)/shard_map/ppermute | solution.py:498
  60.1 5.6 %collective-permute-start.6 = (f32[9,48,128]{2,1,0:T(8,128)S(1)}, f32[9,48,128]{2,1,0:T(8,128)S(1)}, u32[]{:S(2)}, u32[]{:S(2)}) collective-permute-start(f32[9,48,128]{2,1,0:T(8,128)S(1)} %add_add_fusion.1), channel_id=1, source_target_pairs={{0,12},{1,13},{2,14},{3,15},{4,8},{5,9},{6,10},{7,11},{8,4},{9,5},... | collective-permute-start | bytes 663560 | tf_op jit(solution)/shard_map/ppermute | solution.py:498
  66.2 7.2 %steering.3.refs_11_ = bf16[24,256,512]{2,1,0:T(8,128)(2,1)} custom-call(s32[1]{0:T(128)} %bitcast.1.me_ref, s32[8,240]{1,0:T(8,128)} %constant.36.clone.plan_ref, s32[2,256]{1,0:T(2,128)} %bitcast.34, s32[1,256]{1,0:T(1,128)} %bitcast.38, s32[2,256]{1,0:T(2,128)} %bitcast.36), custom_call_target="tpu_custom_call" | custom-call | flops 40000 | bytes 12600 | tf_op jit(solution)/shard_map/steering/pallas_call | solution.py:338
  73.4 2.9 %collective-permute-done.5 = f32[9,48,128]{2,1,0:T(8,128)S(1)} collective-permute-done((f32[9,48,128]{2,1,0:T(8,128)S(1)}, f32[9,48,128]{2,1,0:T(8,128)S(1)}, u32[]{:S(2)}, u32[]{:S(2)}) %collective-permute-start.5) | collective-permute-done | bytes 221216 | tf_op jit(solution)/shard_map/ppermute | solution.py:498
  76.6 3.0 %collective-permute-start.7 = (f32[8,128]{1,0:T(8,128)S(1)}, f32[8,128]{1,0:T(8,128)S(1)}, u32[]{:S(2)}, u32[]{:S(2)}) collective-permute-start(f32[8,128]{1,0:T(8,128)S(1)} %slice_bitcast_fusion.8), channel_id=1, source_target_pairs={{0,16},{1,17},{2,18},{3,19},{4,20},{5,21},{6,22},{7,23},{8,24},{9,... | collective-permute-start | bytes 12296 | tf_op jit(solution)/shard_map/ppermute | solution.py:498
  79.6 3.0 %collective-permute-start.14 = (f32[48,128]{1,0:T(8,128)S(1)}, f32[48,128]{1,0:T(8,128)S(1)}, u32[]{:S(2)}, u32[]{:S(2)}) collective-permute-start(f32[48,128]{1,0:T(8,128)S(1)} %get-tuple-element.19), channel_id=1, source_target_pairs={{0,224},{32,0},{64,32},{96,64},{128,96},{160,128},{192,160},{224,1... | collective-permute-start | bytes 73736 | tf_op jit(solution)/shard_map/ppermute | solution.py:498
  82.7 2.1 %collective-permute-start.13 = (f32[48,128]{1,0:T(8,128)S(1)}, f32[48,128]{1,0:T(8,128)S(1)}, u32[]{:S(2)}, u32[]{:S(2)}) collective-permute-start(f32[48,128]{1,0:T(8,128)S(1)} %get-tuple-element.20), channel_id=1, source_target_pairs={{0,192},{32,224},{64,0},{96,32},{128,64},{160,96},{192,128},{224,1... | collective-permute-start | bytes 73736 | tf_op jit(solution)/shard_map/ppermute | solution.py:498
  84.8 1.2 collective-permute-start.12
  85.9 3.3 %collective-permute-start.11 = (f32[48,128]{1,0:T(8,128)S(1)}, f32[48,128]{1,0:T(8,128)S(1)}, u32[]{:S(2)}, u32[]{:S(2)}) collective-permute-start(f32[48,128]{1,0:T(8,128)S(1)} %get-tuple-element.22), channel_id=1, source_target_pairs={{0,128},{32,160},{64,192},{96,224},{128,0},{160,32},{192,64},{224,... | collective-permute-start | bytes 73736 | tf_op jit(solution)/shard_map/ppermute | solution.py:498
  89.3 3.2 %collective-permute-start.9 = (f32[48,128]{1,0:T(8,128)S(1)}, f32[48,128]{1,0:T(8,128)S(1)}, u32[]{:S(2)}, u32[]{:S(2)}) collective-permute-start(f32[48,128]{1,0:T(8,128)S(1)} %get-tuple-element.24), channel_id=1, source_target_pairs={{0,64},{32,96},{64,128},{96,160},{128,192},{160,224},{192,0},{224,... | collective-permute-start | bytes 73736 | tf_op jit(solution)/shard_map/ppermute | solution.py:498
  92.5 1.2 collective-permute-start.8
  93.7 1.5 %collective-permute-done.10.refs_3_ = f32[48,128]{1,0:T(8,128)S(1)} collective-permute-done((f32[48,128]{1,0:T(8,128)S(1)}, f32[48,128]{1,0:T(8,128)S(1)}, u32[]{:S(2)}, u32[]{:S(2)}) %collective-permute-start.10) | collective-permute-done | bytes 24608 | tf_op jit(solution)/shard_map/ppermute | solution.py:498
  95.2 1.7 %collective-permute-done.8.refs_1_ = f32[48,128]{1,0:T(8,128)S(1)} collective-permute-done((f32[48,128]{1,0:T(8,128)S(1)}, f32[48,128]{1,0:T(8,128)S(1)}, u32[]{:S(2)}, u32[]{:S(2)}) %collective-permute-start.8) | collective-permute-done | bytes 24608 | tf_op jit(solution)/shard_map/ppermute | solution.py:498
  97.0 9.2 %beams.1 = f32[32,8,128]{2,1,0:T(8,128)S(1)} custom-call(s32[1]{0:T(128)} %bitcast.1.me_ref, s32[8,240]{1,0:T(8,128)S(1)} %copy-done, f32[384]{0:T(512)S(1)} %slice_bitcast_fusion.9.tol_ref, f32[48,128]{1,0:T(8,128)S(1)} %get-tuple-element.26.refs_0_, f32[48,128]{1,0:T(8,128)S(1)} %collective-permute-done.8.refs_1_, ...), custom_call_target="tpu_custom_call" | custom-call | flops 2400000000 | bytes 16000000 | tf_op jit(solution)/shard_map/beams/pallas_call | solution.py:448
  106.2 23.1 %all_to_all.10 = f32[256,1,128]{2,1,0:T(1,128)} all-to-all(f32[256,1,128]{2,1,0:T(1,128)S(1)} %bitcast.31), channel_id=1, replica_groups=mesh['stn'=8,'tm'=32] {'tm','stn'}, dimensions={0} | all-to-all | bytes 262144 | tf_op jit(solution)/shard_map/all_to_all | solution.py:541
  129.3 1.7 %settle.1 = f32[12,32,32]{2,1,0:T(8,128)} custom-call(s32[1]{0:T(128)} %bitcast.t_ref, f32[256,128]{1,0:T(8,128)} %bitcast.32), custom_call_target="tpu_custom_call" | custom-call | tf_op jit(solution)/shard_map/settle/pallas_call | solution.py:480
  (30 shorter events, 1.6 us)
Async XLA Ops:
  0.0 19.8 %copy-start.1 = (f32[12]{0:T(128)S(1)}, f32[12]{0:T(128)}, u32[]{:S(2)}) copy-start(f32[12]{0:T(128)} %param.11) | copy-start | bytes 148
  15.3 21.9 %collective-permute-start = (bf16[8,8,96,128]{3,2,1,0:T(8,128)(2,1)S(1)}, bf16[8,8,96,128]{3,2,1,0:T(8,128)(2,1)S(1)}, u32[]{:S(2)}, u32[]{:S(2)}) collective-permute-start(bf16[8,8,96,128]{3,2,1,0:T(8,128)(2,1)S(1)} %carried.1), channel_id=1, source_target_pairs={{0,1},{1,2},{2,3},{3,4},{4,5},{5,6},{6,7},{7,8},{8,9},{9,10},{10,1... | collective-permute-start | bytes 4718600 | tf_op jit(solution)/shard_map/ppermute | solution.py:520
  40.1 56.9 %all-to-all-start = ((bf16[8,8,96,128]{3,2,1,0:T(8,128)(2,1)}), bf16[8,8,96,128]{3,2,1,0:T(8,128)(2,1)S(1)}, u32[]{:S(2)}, u32[]{:S(2)}) async-start(bf16[8,8,96,128]{3,2,1,0:T(8,128)(2,1)} %get-tuple-element.14), calls=%async_computation | async-start | bytes 3145728 | tf_op jit(solution)/shard_map/all_to_all | solution.py:490
  48.3 10.1 %collective-permute-start.3 = (f32[9,48,128]{2,1,0:T(8,128)S(1)}, f32[9,48,128]{2,1,0:T(8,128)S(1)}, u32[]{:S(2)}, u32[]{:S(2)}) collective-permute-start(f32[9,48,128]{2,1,0:T(8,128)S(1)} %get-tuple-element.13), channel_id=1, source_target_pairs={{0,3},{1,2},{2,1},{3,0},{4,7},{5,6},{6,5},{7,4},{8,11},{9,10},{10,... | collective-permute-start | bytes 663560 | tf_op jit(solution)/shard_map/ppermute | solution.py:498
  51.0 9.0 %collective-permute-start.2 = (f32[9,48,128]{2,1,0:T(8,128)S(1)}, f32[9,48,128]{2,1,0:T(8,128)S(1)}, u32[]{:S(2)}, u32[]{:S(2)}) collective-permute-start(f32[9,48,128]{2,1,0:T(8,128)S(1)} %get-tuple-element.13), channel_id=1, source_target_pairs={{0,2},{1,3},{2,0},{3,1},{4,6},{5,7},{6,4},{7,5},{8,10},{9,11},{10,... | collective-permute-start | bytes 663560 | tf_op jit(solution)/shard_map/ppermute | solution.py:498
  51.0 9.0 %collective-permute-start.1 = (f32[9,48,128]{2,1,0:T(8,128)S(1)}, f32[9,48,128]{2,1,0:T(8,128)S(1)}, u32[]{:S(2)}, u32[]{:S(2)}) collective-permute-start(f32[9,48,128]{2,1,0:T(8,128)S(1)} %get-tuple-element.13), channel_id=1, source_target_pairs={{0,1},{1,0},{2,3},{3,2},{4,5},{5,4},{6,7},{7,6},{8,9},{9,8},{10,11... | collective-permute-start | bytes 663560 | tf_op jit(solution)/shard_map/ppermute | solution.py:498
  60.1 36.8 %copy-start = (s32[8,240]{1,0:T(8,128)S(1)}, s32[8,240]{1,0:T(8,128)}, u32[]{:S(2)}) copy-start(s32[8,240]{1,0:T(8,128)} %constant.36.clone.plan_ref) | copy-start | bytes 23044
  60.1 13.3 %collective-permute-start.6 = (f32[9,48,128]{2,1,0:T(8,128)S(1)}, f32[9,48,128]{2,1,0:T(8,128)S(1)}, u32[]{:S(2)}, u32[]{:S(2)}) collective-permute-start(f32[9,48,128]{2,1,0:T(8,128)S(1)} %add_add_fusion.1), channel_id=1, source_target_pairs={{0,12},{1,13},{2,14},{3,15},{4,8},{5,9},{6,10},{7,11},{8,4},{9,5},... | collective-permute-start | bytes 663560 | tf_op jit(solution)/shard_map/ppermute | solution.py:498
  65.7 10.6 %collective-permute-start.5 = (f32[9,48,128]{2,1,0:T(8,128)S(1)}, f32[9,48,128]{2,1,0:T(8,128)S(1)}, u32[]{:S(2)}, u32[]{:S(2)}) collective-permute-start(f32[9,48,128]{2,1,0:T(8,128)S(1)} %add_add_fusion.1), channel_id=1, source_target_pairs={{0,8},{1,9},{2,10},{3,11},{4,12},{5,13},{6,14},{7,15},{8,0},{9,1},... | collective-permute-start | bytes 663560 | tf_op jit(solution)/shard_map/ppermute | solution.py:498
  65.9 10.7 %collective-permute-start.4 = (f32[9,48,128]{2,1,0:T(8,128)S(1)}, f32[9,48,128]{2,1,0:T(8,128)S(1)}, u32[]{:S(2)}, u32[]{:S(2)}) collective-permute-start(f32[9,48,128]{2,1,0:T(8,128)S(1)} %add_add_fusion.1), channel_id=1, source_target_pairs={{0,4},{1,5},{2,6},{3,7},{4,0},{5,1},{6,2},{7,3},{8,12},{9,13},{10,... | collective-permute-start | bytes 663560 | tf_op jit(solution)/shard_map/ppermute | solution.py:498
  76.6 12.6 %collective-permute-start.7 = (f32[8,128]{1,0:T(8,128)S(1)}, f32[8,128]{1,0:T(8,128)S(1)}, u32[]{:S(2)}, u32[]{:S(2)}) collective-permute-start(f32[8,128]{1,0:T(8,128)S(1)} %slice_bitcast_fusion.8), channel_id=1, source_target_pairs={{0,16},{1,17},{2,18},{3,19},{4,20},{5,21},{6,22},{7,23},{8,24},{9,... | collective-permute-start | bytes 12296 | tf_op jit(solution)/shard_map/ppermute | solution.py:498
  79.6 9.6 %collective-permute-start.14 = (f32[48,128]{1,0:T(8,128)S(1)}, f32[48,128]{1,0:T(8,128)S(1)}, u32[]{:S(2)}, u32[]{:S(2)}) collective-permute-start(f32[48,128]{1,0:T(8,128)S(1)} %get-tuple-element.19), channel_id=1, source_target_pairs={{0,224},{32,0},{64,32},{96,64},{128,96},{160,128},{192,160},{224,1... | collective-permute-start | bytes 73736 | tf_op jit(solution)/shard_map/ppermute | solution.py:498
  82.7 9.8 %collective-permute-start.13 = (f32[48,128]{1,0:T(8,128)S(1)}, f32[48,128]{1,0:T(8,128)S(1)}, u32[]{:S(2)}, u32[]{:S(2)}) collective-permute-start(f32[48,128]{1,0:T(8,128)S(1)} %get-tuple-element.20), channel_id=1, source_target_pairs={{0,192},{32,224},{64,0},{96,32},{128,64},{160,96},{192,128},{224,1... | collective-permute-start | bytes 73736 | tf_op jit(solution)/shard_map/ppermute | solution.py:498
  84.8 8.9 %collective-permute-start.12 = (f32[48,128]{1,0:T(8,128)S(1)}, f32[48,128]{1,0:T(8,128)S(1)}, u32[]{:S(2)}, u32[]{:S(2)}) collective-permute-start(f32[48,128]{1,0:T(8,128)S(1)} %get-tuple-element.21), channel_id=1, source_target_pairs={{0,160},{32,192},{64,224},{96,0},{128,32},{160,64},{192,96},{224,1... | collective-permute-start | bytes 73736 | tf_op jit(solution)/shard_map/ppermute | solution.py:498
  85.9 7.8 %collective-permute-start.11 = (f32[48,128]{1,0:T(8,128)S(1)}, f32[48,128]{1,0:T(8,128)S(1)}, u32[]{:S(2)}, u32[]{:S(2)}) collective-permute-start(f32[48,128]{1,0:T(8,128)S(1)} %get-tuple-element.22), channel_id=1, source_target_pairs={{0,128},{32,160},{64,192},{96,224},{128,0},{160,32},{192,64},{224,... | collective-permute-start | bytes 73736 | tf_op jit(solution)/shard_map/ppermute | solution.py:498
  89.2 6.0 %collective-permute-start.10 = (f32[48,128]{1,0:T(8,128)S(1)}, f32[48,128]{1,0:T(8,128)S(1)}, u32[]{:S(2)}, u32[]{:S(2)}) collective-permute-start(f32[48,128]{1,0:T(8,128)S(1)} %get-tuple-element.23), channel_id=1, source_target_pairs={{0,96},{32,128},{64,160},{96,192},{128,224},{160,0},{192,32},{224,... | collective-permute-start | bytes 73736 | tf_op jit(solution)/shard_map/ppermute | solution.py:498
  89.3 6.0 %collective-permute-start.9 = (f32[48,128]{1,0:T(8,128)S(1)}, f32[48,128]{1,0:T(8,128)S(1)}, u32[]{:S(2)}, u32[]{:S(2)}) collective-permute-start(f32[48,128]{1,0:T(8,128)S(1)} %get-tuple-element.24), channel_id=1, source_target_pairs={{0,64},{32,96},{64,128},{96,160},{128,192},{160,224},{192,0},{224,... | collective-permute-start | bytes 73736 | tf_op jit(solution)/shard_map/ppermute | solution.py:498
  92.5 4.4 %collective-permute-start.8 = (f32[48,128]{1,0:T(8,128)S(1)}, f32[48,128]{1,0:T(8,128)S(1)}, u32[]{:S(2)}, u32[]{:S(2)}) collective-permute-start(f32[48,128]{1,0:T(8,128)S(1)} %get-tuple-element.25), channel_id=1, source_target_pairs={{0,32},{32,64},{64,96},{96,128},{128,160},{160,192},{192,224},{224... | collective-permute-start | bytes 73736 | tf_op jit(solution)/shard_map/ppermute | solution.py:498

commit v3 on v2

--- a/solution.py
+++ b/solution.py
@@ -354,16 +354,19 @@
 
 
 def place_stations(in_ref, polar, perm_ref, out_ref):
-    for seg in range(SEGS):
-        stacked = jnp.concatenate([in_ref[g, polar * SEGS + seg] for g in range(N_STN)], 1)
-        moved = jnp.dot(stacked, perm_ref[...], preferred_element_type=F32)
-        for part in range(2):
-            rows = moved[part * LOCAL_CHAN : (part + 1) * LOCAL_CHAN]
-            for f4 in range(4):
+    rows = SEGS * 2 * LOCAL_CHAN
+    own = slice(polar * SEGS, (polar + 1) * SEGS)
+    stacked = jnp.concatenate([in_ref[g, own].reshape(rows, 128) for g in range(N_STN)], 1)
+    for f4 in range(4):
+        columns = slice(f4 * STATIONS, (f4 + 1) * STATIONS)
+        moved = jnp.dot(stacked, perm_ref[:, columns], preferred_element_type=F32)
+        for seg in range(SEGS):
+            for part in range(2):
+                source = (seg * 2 + part) * LOCAL_CHAN
                 at = ((part * 4 + f4) * SEGS + seg) * LOCAL_CHAN
                 for half in range(2):
-                    column = f4 * STATIONS + half * 128
-                    out_ref[half, at : at + LOCAL_CHAN, :] = rows[:, column : column + 128]
+                    piece = moved[source : source + LOCAL_CHAN, half * 128 : half * 128 + 128]
+                    out_ref[half, at : at + LOCAL_CHAN, :] = piece
 
 
 PLACED = (2, 32 * LOCAL_CHAN, 128)
@@ -376,7 +379,7 @@
 def beam_kernel(me_ref, plan_ref, tol_ref, *refs):
     sum_refs = refs[:N_STN]
     in_ref, perm_ref, low_ref, high_ref, out_ref = refs[N_STN : N_STN + 5]
-    window_sums, ordered, first_placed, second_placed, perm, weights, powers, arrival = refs[N_STN + 5 :]
+    window_sums, ordered, first_placed, second_placed, perm, weights, powers, tolerances, softs, arrival = refs[N_STN + 5 :]
 
     def load(chunk):
         source, at = (low_ref, chunk) if chunk < CHUNKS // 2 else (high_ref, chunk - CHUNKS // 2)
@@ -388,6 +391,9 @@
     load_perm.start()
     for chunk in range(CHUNKS):
         load(chunk).start()
+    load_perm.wait()
+    place_stations(in_ref, 0, perm, first_placed)
+    place_stations(in_ref, 1, perm, second_placed)
     powers[...] = jnp.zeros_like(powers)
     lane = lax.broadcasted_iota(jnp.int32, (LOCAL_CHAN, 128), 1)
     for d in range(N_STN):
@@ -404,25 +410,25 @@
                         piece = pltpu.roll(piece, shift, 1)
                     total = jnp.where(lane // 32 == place, piece, total)
                 window_sums[polar, kind, :, half * 128 : half * 128 + 128] = total
-    load_perm.wait()
-    place_stations(in_ref, 0, perm, first_placed)
-    place_stations(in_ref, 1, perm, second_placed)
-
+    for visit in range(LOCAL_CHAN):
+        tolerance = tol_ref[plan_ref[me_ref[0], visit]]
+        row = pl.ds(plan_ref[me_ref[0], 2 * LOCAL_CHAN + visit], 1)
+        tolerances[row, :] = jnp.full((1, STATIONS), tolerance, F32)
     size = float(WINDOW * FRAMES)
+    for polar in range(2):
+        s1, s2 = window_sums[polar, 0], window_sums[polar, 1]
+        kurtosis = (size + 1.0) / (size - 1.0) * (size * s2 / (s1 * s1) - 1.0)
+        deviation = (kurtosis - 1.0) / tolerances[...]
+        softs[polar] = 1.0 / (1.0 + deviation * deviation)
 
     for chunk in range(CHUNKS):
         load(chunk).wait()
         for inner in range(BLOCK):
             visit = chunk * BLOCK + inner
             local = plan_ref[me_ref[0], 2 * LOCAL_CHAN + visit]
-            tolerance = tol_ref[plan_ref[me_ref[0], visit]]
             rows = []
             for polar, ref in enumerate((first_placed, second_placed)):
-                s1 = window_sums[polar, 0, pl.ds(local, 1), :]
-                s2 = window_sums[polar, 1, pl.ds(local, 1), :]
-                kurtosis = (size + 1.0) / (size - 1.0) * (size * s2 / (s1 * s1) - 1.0)
-                deviation = (kurtosis - 1.0) / tolerance
-                soft = 1.0 / (1.0 + deviation * deviation)
+                soft = softs[polar, pl.ds(local, 1), :]
                 halves = [ref[half, pl.ds(local, 32, stride=LOCAL_CHAN), :] for half in range(2)]
                 values = jnp.concatenate(halves, 1)
                 rows.append((values * soft).astype(BF16))
@@ -458,6 +464,8 @@
             pltpu.VMEM(perm.shape, BF16),
             pltpu.VMEM((LOCAL_CHAN, STATIONS, 2 * BEAMS), BF16),
             pltpu.VMEM((2 * N_TM, BEAMS), F32),
+            pltpu.VMEM((LOCAL_CHAN, STATIONS), F32),
+            pltpu.VMEM((2, LOCAL_CHAN, STATIONS), F32),
             pltpu.SemaphoreType.DMA((CHUNKS + 1,)),
         ],
         compiler_params=pltpu.CompilerParams(vmem_limit_bytes=36 * 1024 * 1024),

time: 131 us -> 130 us (level)
  no operation moved by 1% of the time
where the time goes in v3:
time: 130 us
  Pallas kernels  58.4 us (45%)
  starting transfers between devices  39 us (30%)
  blocking collectives  23.1 us (18%)
  waiting for transfers between devices  8.89 us (7%)
    pallas_call x2, Pallas kernels, channelize(): pl.pallas_call(functools.partial(channelize_kernel, carried), out_shape=j...  31.5 us
    ppermute x14, starting transfers between devices, permuted(): lax.ppermute(block, axis, [(i, send_to(i)) for i in range(lax.axis_size(a...  26.3 us
    all_to_all x1, blocking collectives, per_device(): lax.all_to_all(outgoing, ('tm', 'stn'), split_axis=0, concat_axis=0, tile...  23.1 us
    pallas_call x2, Pallas kernels, steering(): pl.pallas_call(functools.partial(steering_kernel, start), out_shape=jax.S...  14.1 us
    all_to_all x1, starting transfers between devices, across_stations(): lax.all_to_all(blocks, 'stn', split_axis=0, concat_axis=0, tiled=True)  8.2 us
    pallas_call x1, Pallas kernels, beams(): pl.pallas_call(beam_kernel, out_shape=jax.ShapeDtypeStruct((N_TM, N_STN,...  8.12 us
    ppermute x14, waiting for transfers between devices, permuted(): lax.ppermute(block, axis, [(i, send_to(i)) for i in range(lax.axis_size(a...  8.02 us
    ppermute x1, starting transfers between devices, per_device(): received = lax.ppermute(leaving, 'tm', shift)  4.51 us
  transfers between devices with their start and end apart: 16, of which 6 were waited for; matrix products, arithmetic and copies ran while one was open for 0% of the time, Pallas kernels for 23%

profile of v3, /device:TPU:1, one launch (start us, length us, event | category | flops | bytes accessed | tf_op | source)
XLA Modules:
  0.0 129.9 jit_solution(9143879197807477045)
XLA Ops:
  0.0 15.3 %carried.1 = bf16[8,8,96,128]{3,2,1,0:T(8,128)(2,1)S(1)} custom-call(bf16[16,2,2,32,2048]{4,3,2,1,0:T(8,128)(2,1)} %refs_3_.2, bf16[16,2,2,32,2048]{4,3,2,1,0:T(8,128)(2,1)} %refs_3_.2, bf16[16,2,2,32,2048]{4,3,2,1,0:T(8,128)(2,1)} %refs_3_.2, bf16[16,2,2,32,2048]{4,3,2,1,0:T(8,128)(2,1)} %refs_3_.2, f32[16,2048]{1,0:T(8,128)} %refs_7_.3, ...), custom_call_target="tpu_custom_call" | custom-call | flops 14000000000 | bytes 16000000 | tf_op jit(solution)/shard_map/carried/pallas_call | solution.py:197
  15.3 4.5 %collective-permute-start = (bf16[8,8,96,128]{3,2,1,0:T(8,128)(2,1)S(1)}, bf16[8,8,96,128]{3,2,1,0:T(8,128)(2,1)S(1)}, u32[]{:S(2)}, u32[]{:S(2)}) collective-permute-start(bf16[8,8,96,128]{3,2,1,0:T(8,128)(2,1)S(1)} %carried.1), channel_id=1, source_target_pairs={{0,1},{1,2},{2,3},{3,4},{4,5},{5,6},{6,7},{7,8},{8,9},{9,10},{10,1... | collective-permute-start | bytes 4718600 | tf_op jit(solution)/shard_map/ppermute | solution.py:528
  19.9 16.3 %own.1.own_ref = f32[8,8,96,128]{3,2,1,0:T(8,128)S(1)} custom-call(bf16[16,2,2,32,2048]{4,3,2,1,0:T(8,128)(2,1)} %refs_3_.2, bf16[16,2,2,32,2048]{4,3,2,1,0:T(8,128)(2,1)} %refs_3_.2, bf16[16,2,2,32,2048]{4,3,2,1,0:T(8,128)(2,1)} %refs_3_.2, bf16[16,2,2,32,2048]{4,3,2,1,0:T(8,128)(2,1)} %refs_3_.2, f32[16,2048]{1,0:T(8,128)} %refs_7_.3, f32[16,2048]{1,0:T(8,128)} %refs_7_.3, ...), custom_call_target="tpu_custom_call" | custom-call | flops 14000000000 | bytes 16000000 | tf_op jit(solution)/shard_map/own/pallas_call | solution.py:197
  36.2 0.9 collective-permute-done.received_ref
  37.1 2.9 %combine.1 = (bf16[8,8,96,128]{3,2,1,0:T(8,128)(2,1)}, f32[9,48,128]{2,1,0:T(8,128)S(1)}) custom-call(s32[1]{0:T(128)} %bitcast.1.me_ref, f32[8,8,96,128]{3,2,1,0:T(8,128)S(1)} %own.1.own_ref, bf16[8,8,96,128]{3,2,1,0:T(8,128)(2,1)S(1)} %collective-permute-done.received_ref, f32[48,128]{1,0:T(8,128)S(1)} %pad.4.tol_ref), custom_call_target="tpu_custom_call" | custom-call | flops 8000000 | bytes 8000000 | tf_op jit(solution)/shard_map/combine/pallas_call | solution.py:246
  40.1 8.2 %all-to-all-start = ((bf16[8,8,96,128]{3,2,1,0:T(8,128)(2,1)}), bf16[8,8,96,128]{3,2,1,0:T(8,128)(2,1)S(1)}, u32[]{:S(2)}, u32[]{:S(2)}) async-start(bf16[8,8,96,128]{3,2,1,0:T(8,128)(2,1)} %get-tuple-element.14), calls=%async_computation | async-start | bytes 3145728 | tf_op jit(solution)/shard_map/all_to_all | solution.py:498
  48.3 2.8 %collective-permute-start.3 = (f32[9,48,128]{2,1,0:T(8,128)S(1)}, f32[9,48,128]{2,1,0:T(8,128)S(1)}, u32[]{:S(2)}, u32[]{:S(2)}) collective-permute-start(f32[9,48,128]{2,1,0:T(8,128)S(1)} %get-tuple-element.13), channel_id=1, source_target_pairs={{0,3},{1,2},{2,1},{3,0},{4,7},{5,6},{6,5},{7,4},{8,11},{9,10},{10,... | collective-permute-start | bytes 663560 | tf_op jit(solution)/shard_map/ppermute | solution.py:506
  51.5 6.9 %steering.2.refs_10_ = bf16[24,256,512]{2,1,0:T(8,128)(2,1)} custom-call(s32[1]{0:T(128)} %bitcast.1.me_ref, s32[8,240]{1,0:T(8,128)} %constant.36.clone.plan_ref, s32[2,256]{1,0:T(2,128)} %bitcast.33, s32[1,256]{1,0:T(1,128)} %bitcast.37, s32[2,256]{1,0:T(2,128)} %bitcast.35), custom_call_target="tpu_custom_call" | custom-call | flops 40000 | bytes 12600 | tf_op jit(solution)/shard_map/steering/pallas_call | solution.py:338
  58.4 1.6 %collective-permute-done.2 = f32[9,48,128]{2,1,0:T(8,128)S(1)} collective-permute-done((f32[9,48,128]{2,1,0:T(8,128)S(1)}, f32[9,48,128]{2,1,0:T(8,128)S(1)}, u32[]{:S(2)}, u32[]{:S(2)}) %collective-permute-start.2) | collective-permute-done | bytes 221216 | tf_op jit(solution)/shard_map/ppermute | solution.py:506
  60.1 5.6 %collective-permute-start.6 = (f32[9,48,128]{2,1,0:T(8,128)S(1)}, f32[9,48,128]{2,1,0:T(8,128)S(1)}, u32[]{:S(2)}, u32[]{:S(2)}) collective-permute-start(f32[9,48,128]{2,1,0:T(8,128)S(1)} %add_add_fusion.1), channel_id=1, source_target_pairs={{0,12},{1,13},{2,14},{3,15},{4,8},{5,9},{6,10},{7,11},{8,4},{9,5},... | collective-permute-start | bytes 663560 | tf_op jit(solution)/shard_map/ppermute | solution.py:506
  66.2 7.2 %steering.3.refs_11_ = bf16[24,256,512]{2,1,0:T(8,128)(2,1)} custom-call(s32[1]{0:T(128)} %bitcast.1.me_ref, s32[8,240]{1,0:T(8,128)} %constant.36.clone.plan_ref, s32[2,256]{1,0:T(2,128)} %bitcast.34, s32[1,256]{1,0:T(1,128)} %bitcast.38, s32[2,256]{1,0:T(2,128)} %bitcast.36), custom_call_target="tpu_custom_call" | custom-call | flops 40000 | bytes 12600 | tf_op jit(solution)/shard_map/steering/pallas_call | solution.py:338
  73.4 2.9 %collective-permute-done.5 = f32[9,48,128]{2,1,0:T(8,128)S(1)} collective-permute-done((f32[9,48,128]{2,1,0:T(8,128)S(1)}, f32[9,48,128]{2,1,0:T(8,128)S(1)}, u32[]{:S(2)}, u32[]{:S(2)}) %collective-permute-start.5) | collective-permute-done | bytes 221216 | tf_op jit(solution)/shard_map/ppermute | solution.py:506
  76.6 3.0 %collective-permute-start.7 = (f32[8,128]{1,0:T(8,128)S(1)}, f32[8,128]{1,0:T(8,128)S(1)}, u32[]{:S(2)}, u32[]{:S(2)}) collective-permute-start(f32[8,128]{1,0:T(8,128)S(1)} %slice_bitcast_fusion.8), channel_id=1, source_target_pairs={{0,16},{1,17},{2,18},{3,19},{4,20},{5,21},{6,22},{7,23},{8,24},{9,... | collective-permute-start | bytes 12296 | tf_op jit(solution)/shard_map/ppermute | solution.py:506
  79.6 3.0 %collective-permute-start.14 = (f32[48,128]{1,0:T(8,128)S(1)}, f32[48,128]{1,0:T(8,128)S(1)}, u32[]{:S(2)}, u32[]{:S(2)}) collective-permute-start(f32[48,128]{1,0:T(8,128)S(1)} %get-tuple-element.19), channel_id=1, source_target_pairs={{0,224},{32,0},{64,32},{96,64},{128,96},{160,128},{192,160},{224,1... | collective-permute-start | bytes 73736 | tf_op jit(solution)/shard_map/ppermute | solution.py:506
  82.7 2.1 %collective-permute-start.13 = (f32[48,128]{1,0:T(8,128)S(1)}, f32[48,128]{1,0:T(8,128)S(1)}, u32[]{:S(2)}, u32[]{:S(2)}) collective-permute-start(f32[48,128]{1,0:T(8,128)S(1)} %get-tuple-element.20), channel_id=1, source_target_pairs={{0,192},{32,224},{64,0},{96,32},{128,64},{160,96},{192,128},{224,1... | collective-permute-start | bytes 73736 | tf_op jit(solution)/shard_map/ppermute | solution.py:506
  84.8 1.2 collective-permute-start.12
  85.9 3.3 %collective-permute-start.11 = (f32[48,128]{1,0:T(8,128)S(1)}, f32[48,128]{1,0:T(8,128)S(1)}, u32[]{:S(2)}, u32[]{:S(2)}) collective-permute-start(f32[48,128]{1,0:T(8,128)S(1)} %get-tuple-element.22), channel_id=1, source_target_pairs={{0,128},{32,160},{64,192},{96,224},{128,0},{160,32},{192,64},{224,... | collective-permute-start | bytes 73736 | tf_op jit(solution)/shard_map/ppermute | solution.py:506
  89.3 3.2 %collective-permute-start.9 = (f32[48,128]{1,0:T(8,128)S(1)}, f32[48,128]{1,0:T(8,128)S(1)}, u32[]{:S(2)}, u32[]{:S(2)}) collective-permute-start(f32[48,128]{1,0:T(8,128)S(1)} %get-tuple-element.24), channel_id=1, source_target_pairs={{0,64},{32,96},{64,128},{96,160},{128,192},{160,224},{192,0},{224,... | collective-permute-start | bytes 73736 | tf_op jit(solution)/shard_map/ppermute | solution.py:506
  92.5 1.2 collective-permute-start.8
  93.7 1.5 %collective-permute-done.10.refs_3_ = f32[48,128]{1,0:T(8,128)S(1)} collective-permute-done((f32[48,128]{1,0:T(8,128)S(1)}, f32[48,128]{1,0:T(8,128)S(1)}, u32[]{:S(2)}, u32[]{:S(2)}) %collective-permute-start.10) | collective-permute-done | bytes 24608 | tf_op jit(solution)/shard_map/ppermute | solution.py:506
  95.2 1.7 %collective-permute-done.8.refs_1_ = f32[48,128]{1,0:T(8,128)S(1)} collective-permute-done((f32[48,128]{1,0:T(8,128)S(1)}, f32[48,128]{1,0:T(8,128)S(1)}, u32[]{:S(2)}, u32[]{:S(2)}) %collective-permute-start.8) | collective-permute-done | bytes 24608 | tf_op jit(solution)/shard_map/ppermute | solution.py:506
  97.0 8.1 %beams.1 = f32[32,8,128]{2,1,0:T(8,128)S(1)} custom-call(s32[1]{0:T(128)} %bitcast.1.me_ref, s32[8,240]{1,0:T(8,128)S(1)} %copy-done, f32[384]{0:T(512)S(1)} %slice_bitcast_fusion.9.tol_ref, f32[48,128]{1,0:T(8,128)S(1)} %get-tuple-element.26.refs_0_, f32[48,128]{1,0:T(8,128)S(1)} %collective-permute-done.8.refs_1_, ...), custom_call_target="tpu_custom_call" | custom-call | flops 2400000000 | bytes 16000000 | tf_op jit(solution)/shard_map/beams/pallas_call | solution.py:454
  105.1 23.1 %all_to_all.10 = f32[256,1,128]{2,1,0:T(1,128)} all-to-all(f32[256,1,128]{2,1,0:T(1,128)S(1)} %bitcast.31), channel_id=1, replica_groups=mesh['stn'=8,'tm'=32] {'tm','stn'}, dimensions={0} | all-to-all | bytes 262144 | tf_op jit(solution)/shard_map/all_to_all | solution.py:549
  128.2 1.7 %settle.1 = f32[12,32,32]{2,1,0:T(8,128)} custom-call(s32[1]{0:T(128)} %bitcast.t_ref, f32[256,128]{1,0:T(8,128)} %bitcast.32), custom_call_target="tpu_custom_call" | custom-call | tf_op jit(solution)/shard_map/settle/pallas_call | solution.py:488
  (30 shorter events, 1.6 us)
Async XLA Ops:
  0.0 19.8 %copy-start.1 = (f32[12]{0:T(128)S(1)}, f32[12]{0:T(128)}, u32[]{:S(2)}) copy-start(f32[12]{0:T(128)} %param.11) | copy-start | bytes 148
  15.3 21.9 %collective-permute-start = (bf16[8,8,96,128]{3,2,1,0:T(8,128)(2,1)S(1)}, bf16[8,8,96,128]{3,2,1,0:T(8,128)(2,1)S(1)}, u32[]{:S(2)}, u32[]{:S(2)}) collective-permute-start(bf16[8,8,96,128]{3,2,1,0:T(8,128)(2,1)S(1)} %carried.1), channel_id=1, source_target_pairs={{0,1},{1,2},{2,3},{3,4},{4,5},{5,6},{6,7},{7,8},{8,9},{9,10},{10,1... | collective-permute-start | bytes 4718600 | tf_op jit(solution)/shard_map/ppermute | solution.py:528
  40.1 56.9 %all-to-all-start = ((bf16[8,8,96,128]{3,2,1,0:T(8,128)(2,1)}), bf16[8,8,96,128]{3,2,1,0:T(8,128)(2,1)S(1)}, u32[]{:S(2)}, u32[]{:S(2)}) async-start(bf16[8,8,96,128]{3,2,1,0:T(8,128)(2,1)} %get-tuple-element.14), calls=%async_computation | async-start | bytes 3145728 | tf_op jit(solution)/shard_map/all_to_all | solution.py:498
  48.3 10.1 %collective-permute-start.3 = (f32[9,48,128]{2,1,0:T(8,128)S(1)}, f32[9,48,128]{2,1,0:T(8,128)S(1)}, u32[]{:S(2)}, u32[]{:S(2)}) collective-permute-start(f32[9,48,128]{2,1,0:T(8,128)S(1)} %get-tuple-element.13), channel_id=1, source_target_pairs={{0,3},{1,2},{2,1},{3,0},{4,7},{5,6},{6,5},{7,4},{8,11},{9,10},{10,... | collective-permute-start | bytes 663560 | tf_op jit(solution)/shard_map/ppermute | solution.py:506
  51.0 9.0 %collective-permute-start.2 = (f32[9,48,128]{2,1,0:T(8,128)S(1)}, f32[9,48,128]{2,1,0:T(8,128)S(1)}, u32[]{:S(2)}, u32[]{:S(2)}) collective-permute-start(f32[9,48,128]{2,1,0:T(8,128)S(1)} %get-tuple-element.13), channel_id=1, source_target_pairs={{0,2},{1,3},{2,0},{3,1},{4,6},{5,7},{6,4},{7,5},{8,10},{9,11},{10,... | collective-permute-start | bytes 663560 | tf_op jit(solution)/shard_map/ppermute | solution.py:506
  51.0 9.0 %collective-permute-start.1 = (f32[9,48,128]{2,1,0:T(8,128)S(1)}, f32[9,48,128]{2,1,0:T(8,128)S(1)}, u32[]{:S(2)}, u32[]{:S(2)}) collective-permute-start(f32[9,48,128]{2,1,0:T(8,128)S(1)} %get-tuple-element.13), channel_id=1, source_target_pairs={{0,1},{1,0},{2,3},{3,2},{4,5},{5,4},{6,7},{7,6},{8,9},{9,8},{10,11... | collective-permute-start | bytes 663560 | tf_op jit(solution)/shard_map/ppermute | solution.py:506
  60.1 36.8 %copy-start = (s32[8,240]{1,0:T(8,128)S(1)}, s32[8,240]{1,0:T(8,128)}, u32[]{:S(2)}) copy-start(s32[8,240]{1,0:T(8,128)} %constant.36.clone.plan_ref) | copy-start | bytes 23044
  60.1 13.3 %collective-permute-start.6 = (f32[9,48,128]{2,1,0:T(8,128)S(1)}, f32[9,48,128]{2,1,0:T(8,128)S(1)}, u32[]{:S(2)}, u32[]{:S(2)}) collective-permute-start(f32[9,48,128]{2,1,0:T(8,128)S(1)} %add_add_fusion.1), channel_id=1, source_target_pairs={{0,12},{1,13},{2,14},{3,15},{4,8},{5,9},{6,10},{7,11},{8,4},{9,5},... | collective-permute-start | bytes 663560 | tf_op jit(solution)/shard_map/ppermute | solution.py:506
  65.7 10.6 %collective-permute-start.5 = (f32[9,48,128]{2,1,0:T(8,128)S(1)}, f32[9,48,128]{2,1,0:T(8,128)S(1)}, u32[]{:S(2)}, u32[]{:S(2)}) collective-permute-start(f32[9,48,128]{2,1,0:T(8,128)S(1)} %add_add_fusion.1), channel_id=1, source_target_pairs={{0,8},{1,9},{2,10},{3,11},{4,12},{5,13},{6,14},{7,15},{8,0},{9,1},... | collective-permute-start | bytes 663560 | tf_op jit(solution)/shard_map/ppermute | solution.py:506
  65.9 10.7 %collective-permute-start.4 = (f32[9,48,128]{2,1,0:T(8,128)S(1)}, f32[9,48,128]{2,1,0:T(8,128)S(1)}, u32[]{:S(2)}, u32[]{:S(2)}) collective-permute-start(f32[9,48,128]{2,1,0:T(8,128)S(1)} %add_add_fusion.1), channel_id=1, source_target_pairs={{0,4},{1,5},{2,6},{3,7},{4,0},{5,1},{6,2},{7,3},{8,12},{9,13},{10,... | collective-permute-start | bytes 663560 | tf_op jit(solution)/shard_map/ppermute | solution.py:506
  76.6 12.6 %collective-permute-start.7 = (f32[8,128]{1,0:T(8,128)S(1)}, f32[8,128]{1,0:T(8,128)S(1)}, u32[]{:S(2)}, u32[]{:S(2)}) collective-permute-start(f32[8,128]{1,0:T(8,128)S(1)} %slice_bitcast_fusion.8), channel_id=1, source_target_pairs={{0,16},{1,17},{2,18},{3,19},{4,20},{5,21},{6,22},{7,23},{8,24},{9,... | collective-permute-start | bytes 12296 | tf_op jit(solution)/shard_map/ppermute | solution.py:506
  79.6 9.6 %collective-permute-start.14 = (f32[48,128]{1,0:T(8,128)S(1)}, f32[48,128]{1,0:T(8,128)S(1)}, u32[]{:S(2)}, u32[]{:S(2)}) collective-permute-start(f32[48,128]{1,0:T(8,128)S(1)} %get-tuple-element.19), channel_id=1, source_target_pairs={{0,224},{32,0},{64,32},{96,64},{128,96},{160,128},{192,160},{224,1... | collective-permute-start | bytes 73736 | tf_op jit(solution)/shard_map/ppermute | solution.py:506
  82.7 9.8 %collective-permute-start.13 = (f32[48,128]{1,0:T(8,128)S(1)}, f32[48,128]{1,0:T(8,128)S(1)}, u32[]{:S(2)}, u32[]{:S(2)}) collective-permute-start(f32[48,128]{1,0:T(8,128)S(1)} %get-tuple-element.20), channel_id=1, source_target_pairs={{0,192},{32,224},{64,0},{96,32},{128,64},{160,96},{192,128},{224,1... | collective-permute-start | bytes 73736 | tf_op jit(solution)/shard_map/ppermute | solution.py:506
  84.8 8.9 %collective-permute-start.12 = (f32[48,128]{1,0:T(8,128)S(1)}, f32[48,128]{1,0:T(8,128)S(1)}, u32[]{:S(2)}, u32[]{:S(2)}) collective-permute-start(f32[48,128]{1,0:T(8,128)S(1)} %get-tuple-element.21), channel_id=1, source_target_pairs={{0,160},{32,192},{64,224},{96,0},{128,32},{160,64},{192,96},{224,1... | collective-permute-start | bytes 73736 | tf_op jit(solution)/shard_map/ppermute | solution.py:506
  85.9 7.8 %collective-permute-start.11 = (f32[48,128]{1,0:T(8,128)S(1)}, f32[48,128]{1,0:T(8,128)S(1)}, u32[]{:S(2)}, u32[]{:S(2)}) collective-permute-start(f32[48,128]{1,0:T(8,128)S(1)} %get-tuple-element.22), channel_id=1, source_target_pairs={{0,128},{32,160},{64,192},{96,224},{128,0},{160,32},{192,64},{224,... | collective-permute-start | bytes 73736 | tf_op jit(solution)/shard_map/ppermute | solution.py:506
  89.2 6.0 %collective-permute-start.10 = (f32[48,128]{1,0:T(8,128)S(1)}, f32[48,128]{1,0:T(8,128)S(1)}, u32[]{:S(2)}, u32[]{:S(2)}) collective-permute-start(f32[48,128]{1,0:T(8,128)S(1)} %get-tuple-element.23), channel_id=1, source_target_pairs={{0,96},{32,128},{64,160},{96,192},{128,224},{160,0},{192,32},{224,... | collective-permute-start | bytes 73736 | tf_op jit(solution)/shard_map/ppermute | solution.py:506
  89.3 6.0 %collective-permute-start.9 = (f32[48,128]{1,0:T(8,128)S(1)}, f32[48,128]{1,0:T(8,128)S(1)}, u32[]{:S(2)}, u32[]{:S(2)}) collective-permute-start(f32[48,128]{1,0:T(8,128)S(1)} %get-tuple-element.24), channel_id=1, source_target_pairs={{0,64},{32,96},{64,128},{96,160},{128,192},{160,224},{192,0},{224,... | collective-permute-start | bytes 73736 | tf_op jit(solution)/shard_map/ppermute | solution.py:506
  92.5 4.4 %collective-permute-start.8 = (f32[48,128]{1,0:T(8,128)S(1)}, f32[48,128]{1,0:T(8,128)S(1)}, u32[]{:S(2)}, u32[]{:S(2)}) collective-permute-start(f32[48,128]{1,0:T(8,128)S(1)} %get-tuple-element.25), channel_id=1, source_target_pairs={{0,32},{32,64},{64,96},{96,128},{128,160},{160,192},{192,224},{224... | collective-permute-start | bytes 73736 | tf_op jit(solution)/shard_map/ppermute | solution.py:506

commit v4 on v3

--- a/solution.py
+++ b/solution.py
@@ -258,7 +258,7 @@
     )(me, own, received, tolerances)
 
 
-STATION_ROWS = 64
+STATION_ROWS = 128
 
 
 def turn(offsets, number):

time: 130 us -> 130 us (level)
  waiting for transfers between devices: 8.89 us -> 5.55 us
  Pallas kernels: 58.4 us -> 61.5 us
    ppermute x14, waiting for transfers between devices: 8.02 us -> 4.67 us  [permuted(): lax.ppermute(block, axis, [(i, send_to(i)) for i in range(lax.axis_size(a...]
    pallas_call x2, Pallas kernels: 14.1 us -> 17.2 us  [steering(): pl.pallas_call(functools.partial(steering_kernel, start), out_shape=jax.S...]
  transfers between devices with their start and end apart: 16 -> 16, of which waited for: 6 -> 5; matrix products, arithmetic and copies ran while one was open for 0% -> 0% of each run, Pallas kernels for 23% -> 26%
where the time goes in v4:
time: 130 us
  Pallas kernels  61.5 us (47%)
  starting transfers between devices  39.5 us (30%)
  blocking collectives  23 us (18%)
  waiting for transfers between devices  5.55 us (4%)
    pallas_call x2, Pallas kernels, channelize(): pl.pallas_call(functools.partial(channelize_kernel, carried), out_shape=j...  31.5 us
    ppermute x14, starting transfers between devices, permuted(): lax.ppermute(block, axis, [(i, send_to(i)) for i in range(lax.axis_size(a...  26.8 us
    all_to_all x1, blocking collectives, per_device(): lax.all_to_all(outgoing, ('tm', 'stn'), split_axis=0, concat_axis=0, tile...  23 us
    pallas_call x2, Pallas kernels, steering(): pl.pallas_call(functools.partial(steering_kernel, start), out_shape=jax.S...  17.2 us
    all_to_all x1, starting transfers between devices, across_stations(): lax.all_to_all(blocks, 'stn', split_axis=0, concat_axis=0, tiled=True)  8.2 us
    pallas_call x1, Pallas kernels, beams(): pl.pallas_call(beam_kernel, out_shape=jax.ShapeDtypeStruct((N_TM, N_STN,...  8.12 us
    ppermute x14, waiting for transfers between devices, permuted(): lax.ppermute(block, axis, [(i, send_to(i)) for i in range(lax.axis_size(a...  4.67 us
    ppermute x1, starting transfers between devices, per_device(): received = lax.ppermute(leaving, 'tm', shift)  4.51 us
  transfers between devices with their start and end apart: 16, of which 5 were waited for; matrix products, arithmetic and copies ran while one was open for 0% of the time, Pallas kernels for 26%

profile of v4, /device:TPU:1, one launch (start us, length us, event | category | flops | bytes accessed | tf_op | source)
XLA Modules:
  0.0 129.9 jit_solution(5625189616231478893)
XLA Ops:
  0.0 15.3 %carried.1 = bf16[8,8,96,128]{3,2,1,0:T(8,128)(2,1)S(1)} custom-call(bf16[16,2,2,32,2048]{4,3,2,1,0:T(8,128)(2,1)} %refs_3_.2, bf16[16,2,2,32,2048]{4,3,2,1,0:T(8,128)(2,1)} %refs_3_.2, bf16[16,2,2,32,2048]{4,3,2,1,0:T(8,128)(2,1)} %refs_3_.2, bf16[16,2,2,32,2048]{4,3,2,1,0:T(8,128)(2,1)} %refs_3_.2, f32[16,2048]{1,0:T(8,128)} %refs_7_.3, ...), custom_call_target="tpu_custom_call" | custom-call | flops 14000000000 | bytes 16000000 | tf_op jit(solution)/shard_map/carried/pallas_call | solution.py:197
  15.3 4.5 %collective-permute-start = (bf16[8,8,96,128]{3,2,1,0:T(8,128)(2,1)S(1)}, bf16[8,8,96,128]{3,2,1,0:T(8,128)(2,1)S(1)}, u32[]{:S(2)}, u32[]{:S(2)}) collective-permute-start(bf16[8,8,96,128]{3,2,1,0:T(8,128)(2,1)S(1)} %carried.1), channel_id=1, source_target_pairs={{0,1},{1,2},{2,3},{3,4},{4,5},{5,6},{6,7},{7,8},{8,9},{9,10},{10,1... | collective-permute-start | bytes 4718600 | tf_op jit(solution)/shard_map/ppermute | solution.py:528
  19.9 16.3 %own.1.own_ref = f32[8,8,96,128]{3,2,1,0:T(8,128)S(1)} custom-call(bf16[16,2,2,32,2048]{4,3,2,1,0:T(8,128)(2,1)} %refs_3_.2, bf16[16,2,2,32,2048]{4,3,2,1,0:T(8,128)(2,1)} %refs_3_.2, bf16[16,2,2,32,2048]{4,3,2,1,0:T(8,128)(2,1)} %refs_3_.2, bf16[16,2,2,32,2048]{4,3,2,1,0:T(8,128)(2,1)} %refs_3_.2, f32[16,2048]{1,0:T(8,128)} %refs_7_.3, f32[16,2048]{1,0:T(8,128)} %refs_7_.3, ...), custom_call_target="tpu_custom_call" | custom-call | flops 14000000000 | bytes 16000000 | tf_op jit(solution)/shard_map/own/pallas_call | solution.py:197
  36.2 0.9 collective-permute-done.received_ref
  37.1 2.9 %combine.1 = (bf16[8,8,96,128]{3,2,1,0:T(8,128)(2,1)}, f32[9,48,128]{2,1,0:T(8,128)S(1)}) custom-call(s32[1]{0:T(128)} %bitcast.1.me_ref, f32[8,8,96,128]{3,2,1,0:T(8,128)S(1)} %own.1.own_ref, bf16[8,8,96,128]{3,2,1,0:T(8,128)(2,1)S(1)} %collective-permute-done.received_ref, f32[48,128]{1,0:T(8,128)S(1)} %pad.4.tol_ref), custom_call_target="tpu_custom_call" | custom-call | flops 8000000 | bytes 8000000 | tf_op jit(solution)/shard_map/combine/pallas_call | solution.py:246
  40.1 8.2 %all-to-all-start = ((bf16[8,8,96,128]{3,2,1,0:T(8,128)(2,1)}), bf16[8,8,96,128]{3,2,1,0:T(8,128)(2,1)S(1)}, u32[]{:S(2)}, u32[]{:S(2)}) async-start(bf16[8,8,96,128]{3,2,1,0:T(8,128)(2,1)} %get-tuple-element.14), calls=%async_computation | async-start | bytes 3145728 | tf_op jit(solution)/shard_map/all_to_all | solution.py:498
  48.3 2.8 %collective-permute-start.3 = (f32[9,48,128]{2,1,0:T(8,128)S(1)}, f32[9,48,128]{2,1,0:T(8,128)S(1)}, u32[]{:S(2)}, u32[]{:S(2)}) collective-permute-start(f32[9,48,128]{2,1,0:T(8,128)S(1)} %get-tuple-element.13), channel_id=1, source_target_pairs={{0,3},{1,2},{2,1},{3,0},{4,7},{5,6},{6,5},{7,4},{8,11},{9,10},{10,... | collective-permute-start | bytes 663560 | tf_op jit(solution)/shard_map/ppermute | solution.py:506
  51.0 0.5 collective-permute-start.1
  51.5 8.4 %steering.2.refs_10_ = bf16[24,256,512]{2,1,0:T(8,128)(2,1)} custom-call(s32[1]{0:T(128)} %bitcast.1.me_ref, s32[8,240]{1,0:T(8,128)} %constant.36.clone.plan_ref, s32[2,256]{1,0:T(2,128)} %bitcast.33, s32[1,256]{1,0:T(1,128)} %bitcast.37, s32[2,256]{1,0:T(2,128)} %bitcast.35), custom_call_target="tpu_custom_call" | custom-call | flops 40000 | bytes 12600 | tf_op jit(solution)/shard_map/steering/pallas_call | solution.py:338
  60.1 5.6 %collective-permute-start.6 = (f32[9,48,128]{2,1,0:T(8,128)S(1)}, f32[9,48,128]{2,1,0:T(8,128)S(1)}, u32[]{:S(2)}, u32[]{:S(2)}) collective-permute-start(f32[9,48,128]{2,1,0:T(8,128)S(1)} %add_add_fusion.1), channel_id=1, source_target_pairs={{0,12},{1,13},{2,14},{3,15},{4,8},{5,9},{6,10},{7,11},{8,4},{9,5},... | collective-permute-start | bytes 663560 | tf_op jit(solution)/shard_map/ppermute | solution.py:506
  66.3 8.8 %steering.3.refs_11_ = bf16[24,256,512]{2,1,0:T(8,128)(2,1)} custom-call(s32[1]{0:T(128)} %bitcast.1.me_ref, s32[8,240]{1,0:T(8,128)} %constant.36.clone.plan_ref, s32[2,256]{1,0:T(2,128)} %bitcast.34, s32[1,256]{1,0:T(1,128)} %bitcast.38, s32[2,256]{1,0:T(2,128)} %bitcast.36), custom_call_target="tpu_custom_call" | custom-call | flops 40000 | bytes 12600 | tf_op jit(solution)/shard_map/steering/pallas_call | solution.py:338
  75.1 1.2 collective-permute-done.5
  76.4 3.4 %collective-permute-start.7 = (f32[8,128]{1,0:T(8,128)S(1)}, f32[8,128]{1,0:T(8,128)S(1)}, u32[]{:S(2)}, u32[]{:S(2)}) collective-permute-start(f32[8,128]{1,0:T(8,128)S(1)} %slice_bitcast_fusion.8), channel_id=1, source_target_pairs={{0,16},{1,17},{2,18},{3,19},{4,20},{5,21},{6,22},{7,23},{8,24},{9,... | collective-permute-start | bytes 12296 | tf_op jit(solution)/shard_map/ppermute | solution.py:506
  79.8 3.0 %collective-permute-start.14 = (f32[48,128]{1,0:T(8,128)S(1)}, f32[48,128]{1,0:T(8,128)S(1)}, u32[]{:S(2)}, u32[]{:S(2)}) collective-permute-start(f32[48,128]{1,0:T(8,128)S(1)} %get-tuple-element.19), channel_id=1, source_target_pairs={{0,224},{32,0},{64,32},{96,64},{128,96},{160,128},{192,160},{224,1... | collective-permute-start | bytes 73736 | tf_op jit(solution)/shard_map/ppermute | solution.py:506
  82.8 2.1 %collective-permute-start.13 = (f32[48,128]{1,0:T(8,128)S(1)}, f32[48,128]{1,0:T(8,128)S(1)}, u32[]{:S(2)}, u32[]{:S(2)}) collective-permute-start(f32[48,128]{1,0:T(8,128)S(1)} %get-tuple-element.20), channel_id=1, source_target_pairs={{0,192},{32,224},{64,0},{96,32},{128,64},{160,96},{192,128},{224,1... | collective-permute-start | bytes 73736 | tf_op jit(solution)/shard_map/ppermute | solution.py:506
  84.9 1.2 collective-permute-start.12
  86.1 3.3 %collective-permute-start.11 = (f32[48,128]{1,0:T(8,128)S(1)}, f32[48,128]{1,0:T(8,128)S(1)}, u32[]{:S(2)}, u32[]{:S(2)}) collective-permute-start(f32[48,128]{1,0:T(8,128)S(1)} %get-tuple-element.22), channel_id=1, source_target_pairs={{0,128},{32,160},{64,192},{96,224},{128,0},{160,32},{192,64},{224,... | collective-permute-start | bytes 73736 | tf_op jit(solution)/shard_map/ppermute | solution.py:506
  89.4 3.2 %collective-permute-start.9 = (f32[48,128]{1,0:T(8,128)S(1)}, f32[48,128]{1,0:T(8,128)S(1)}, u32[]{:S(2)}, u32[]{:S(2)}) collective-permute-start(f32[48,128]{1,0:T(8,128)S(1)} %get-tuple-element.24), channel_id=1, source_target_pairs={{0,64},{32,96},{64,128},{96,160},{128,192},{160,224},{192,0},{224,... | collective-permute-start | bytes 73736 | tf_op jit(solution)/shard_map/ppermute | solution.py:506
  92.7 1.2 collective-permute-start.8
  93.9 1.5 %collective-permute-done.10.refs_3_ = f32[48,128]{1,0:T(8,128)S(1)} collective-permute-done((f32[48,128]{1,0:T(8,128)S(1)}, f32[48,128]{1,0:T(8,128)S(1)}, u32[]{:S(2)}, u32[]{:S(2)}) %collective-permute-start.10) | collective-permute-done | bytes 24608 | tf_op jit(solution)/shard_map/ppermute | solution.py:506
  95.4 1.7 %collective-permute-done.8.refs_1_ = f32[48,128]{1,0:T(8,128)S(1)} collective-permute-done((f32[48,128]{1,0:T(8,128)S(1)}, f32[48,128]{1,0:T(8,128)S(1)}, u32[]{:S(2)}, u32[]{:S(2)}) %collective-permute-start.8) | collective-permute-done | bytes 24608 | tf_op jit(solution)/shard_map/ppermute | solution.py:506
  97.1 8.1 %beams.1 = f32[32,8,128]{2,1,0:T(8,128)S(1)} custom-call(s32[1]{0:T(128)} %bitcast.1.me_ref, s32[8,240]{1,0:T(8,128)S(1)} %copy-done, f32[384]{0:T(512)S(1)} %slice_bitcast_fusion.9.tol_ref, f32[48,128]{1,0:T(8,128)S(1)} %get-tuple-element.26.refs_0_, f32[48,128]{1,0:T(8,128)S(1)} %collective-permute-done.8.refs_1_, ...), custom_call_target="tpu_custom_call" | custom-call | flops 2400000000 | bytes 16000000 | tf_op jit(solution)/shard_map/beams/pallas_call | solution.py:454
  105.3 23.0 %all_to_all.10 = f32[256,1,128]{2,1,0:T(1,128)} all-to-all(f32[256,1,128]{2,1,0:T(1,128)S(1)} %bitcast.31), channel_id=1, replica_groups=mesh['stn'=8,'tm'=32] {'tm','stn'}, dimensions={0} | all-to-all | bytes 262144 | tf_op jit(solution)/shard_map/all_to_all | solution.py:549
  128.2 1.7 %settle.1 = f32[12,32,32]{2,1,0:T(8,128)} custom-call(s32[1]{0:T(128)} %bitcast.t_ref, f32[256,128]{1,0:T(8,128)} %bitcast.32), custom_call_target="tpu_custom_call" | custom-call | tf_op jit(solution)/shard_map/settle/pallas_call | solution.py:488
  (30 shorter events, 1.0 us)
Async XLA Ops:
  0.0 19.8 %copy-start.1 = (f32[12]{0:T(128)S(1)}, f32[12]{0:T(128)}, u32[]{:S(2)}) copy-start(f32[12]{0:T(128)} %param.11) | copy-start | bytes 148
  15.3 21.9 %collective-permute-start = (bf16[8,8,96,128]{3,2,1,0:T(8,128)(2,1)S(1)}, bf16[8,8,96,128]{3,2,1,0:T(8,128)(2,1)S(1)}, u32[]{:S(2)}, u32[]{:S(2)}) collective-permute-start(bf16[8,8,96,128]{3,2,1,0:T(8,128)(2,1)S(1)} %carried.1), channel_id=1, source_target_pairs={{0,1},{1,2},{2,3},{3,4},{4,5},{5,6},{6,7},{7,8},{8,9},{9,10},{10,1... | collective-permute-start | bytes 4718600 | tf_op jit(solution)/shard_map/ppermute | solution.py:528
  40.1 57.1 %all-to-all-start = ((bf16[8,8,96,128]{3,2,1,0:T(8,128)(2,1)}), bf16[8,8,96,128]{3,2,1,0:T(8,128)(2,1)S(1)}, u32[]{:S(2)}, u32[]{:S(2)}) async-start(bf16[8,8,96,128]{3,2,1,0:T(8,128)(2,1)} %get-tuple-element.14), calls=%async_computation | async-start | bytes 3145728 | tf_op jit(solution)/shard_map/all_to_all | solution.py:498
  48.3 11.6 %collective-permute-start.3 = (f32[9,48,128]{2,1,0:T(8,128)S(1)}, f32[9,48,128]{2,1,0:T(8,128)S(1)}, u32[]{:S(2)}, u32[]{:S(2)}) collective-permute-start(f32[9,48,128]{2,1,0:T(8,128)S(1)} %get-tuple-element.13), channel_id=1, source_target_pairs={{0,3},{1,2},{2,1},{3,0},{4,7},{5,6},{6,5},{7,4},{8,11},{9,10},{10,... | collective-permute-start | bytes 663560 | tf_op jit(solution)/shard_map/ppermute | solution.py:506
  51.0 9.0 %collective-permute-start.2 = (f32[9,48,128]{2,1,0:T(8,128)S(1)}, f32[9,48,128]{2,1,0:T(8,128)S(1)}, u32[]{:S(2)}, u32[]{:S(2)}) collective-permute-start(f32[9,48,128]{2,1,0:T(8,128)S(1)} %get-tuple-element.13), channel_id=1, source_target_pairs={{0,2},{1,3},{2,0},{3,1},{4,6},{5,7},{6,4},{7,5},{8,10},{9,11},{10,... | collective-permute-start | bytes 663560 | tf_op jit(solution)/shard_map/ppermute | solution.py:506
  51.0 9.0 %collective-permute-start.1 = (f32[9,48,128]{2,1,0:T(8,128)S(1)}, f32[9,48,128]{2,1,0:T(8,128)S(1)}, u32[]{:S(2)}, u32[]{:S(2)}) collective-permute-start(f32[9,48,128]{2,1,0:T(8,128)S(1)} %get-tuple-element.13), channel_id=1, source_target_pairs={{0,1},{1,0},{2,3},{3,2},{4,5},{5,4},{6,7},{7,6},{8,9},{9,8},{10,11... | collective-permute-start | bytes 663560 | tf_op jit(solution)/shard_map/ppermute | solution.py:506
  60.1 37.0 %copy-start = (s32[8,240]{1,0:T(8,128)S(1)}, s32[8,240]{1,0:T(8,128)}, u32[]{:S(2)}) copy-start(s32[8,240]{1,0:T(8,128)} %constant.36.clone.plan_ref) | copy-start | bytes 23044
  60.1 15.0 %collective-permute-start.6 = (f32[9,48,128]{2,1,0:T(8,128)S(1)}, f32[9,48,128]{2,1,0:T(8,128)S(1)}, u32[]{:S(2)}, u32[]{:S(2)}) collective-permute-start(f32[9,48,128]{2,1,0:T(8,128)S(1)} %add_add_fusion.1), channel_id=1, source_target_pairs={{0,12},{1,13},{2,14},{3,15},{4,8},{5,9},{6,10},{7,11},{8,4},{9,5},... | collective-permute-start | bytes 663560 | tf_op jit(solution)/shard_map/ppermute | solution.py:506
  65.7 10.6 %collective-permute-start.5 = (f32[9,48,128]{2,1,0:T(8,128)S(1)}, f32[9,48,128]{2,1,0:T(8,128)S(1)}, u32[]{:S(2)}, u32[]{:S(2)}) collective-permute-start(f32[9,48,128]{2,1,0:T(8,128)S(1)} %add_add_fusion.1), channel_id=1, source_target_pairs={{0,8},{1,9},{2,10},{3,11},{4,12},{5,13},{6,14},{7,15},{8,0},{9,1},... | collective-permute-start | bytes 663560 | tf_op jit(solution)/shard_map/ppermute | solution.py:506
  65.9 10.5 %collective-permute-start.4 = (f32[9,48,128]{2,1,0:T(8,128)S(1)}, f32[9,48,128]{2,1,0:T(8,128)S(1)}, u32[]{:S(2)}, u32[]{:S(2)}) collective-permute-start(f32[9,48,128]{2,1,0:T(8,128)S(1)} %add_add_fusion.1), channel_id=1, source_target_pairs={{0,4},{1,5},{2,6},{3,7},{4,0},{5,1},{6,2},{7,3},{8,12},{9,13},{10,... | collective-permute-start | bytes 663560 | tf_op jit(solution)/shard_map/ppermute | solution.py:506
  76.4 13.0 %collective-permute-start.7 = (f32[8,128]{1,0:T(8,128)S(1)}, f32[8,128]{1,0:T(8,128)S(1)}, u32[]{:S(2)}, u32[]{:S(2)}) collective-permute-start(f32[8,128]{1,0:T(8,128)S(1)} %slice_bitcast_fusion.8), channel_id=1, source_target_pairs={{0,16},{1,17},{2,18},{3,19},{4,20},{5,21},{6,22},{7,23},{8,24},{9,... | collective-permute-start | bytes 12296 | tf_op jit(solution)/shard_map/ppermute | solution.py:506
  79.8 9.6 %collective-permute-start.14 = (f32[48,128]{1,0:T(8,128)S(1)}, f32[48,128]{1,0:T(8,128)S(1)}, u32[]{:S(2)}, u32[]{:S(2)}) collective-permute-start(f32[48,128]{1,0:T(8,128)S(1)} %get-tuple-element.19), channel_id=1, source_target_pairs={{0,224},{32,0},{64,32},{96,64},{128,96},{160,128},{192,160},{224,1... | collective-permute-start | bytes 73736 | tf_op jit(solution)/shard_map/ppermute | solution.py:506
  82.8 9.8 %collective-permute-start.13 = (f32[48,128]{1,0:T(8,128)S(1)}, f32[48,128]{1,0:T(8,128)S(1)}, u32[]{:S(2)}, u32[]{:S(2)}) collective-permute-start(f32[48,128]{1,0:T(8,128)S(1)} %get-tuple-element.20), channel_id=1, source_target_pairs={{0,192},{32,224},{64,0},{96,32},{128,64},{160,96},{192,128},{224,1... | collective-permute-start | bytes 73736 | tf_op jit(solution)/shard_map/ppermute | solution.py:506
  84.9 8.9 %collective-permute-start.12 = (f32[48,128]{1,0:T(8,128)S(1)}, f32[48,128]{1,0:T(8,128)S(1)}, u32[]{:S(2)}, u32[]{:S(2)}) collective-permute-start(f32[48,128]{1,0:T(8,128)S(1)} %get-tuple-element.21), channel_id=1, source_target_pairs={{0,160},{32,192},{64,224},{96,0},{128,32},{160,64},{192,96},{224,1... | collective-permute-start | bytes 73736 | tf_op jit(solution)/shard_map/ppermute | solution.py:506
  86.1 7.8 %collective-permute-start.11 = (f32[48,128]{1,0:T(8,128)S(1)}, f32[48,128]{1,0:T(8,128)S(1)}, u32[]{:S(2)}, u32[]{:S(2)}) collective-permute-start(f32[48,128]{1,0:T(8,128)S(1)} %get-tuple-element.22), channel_id=1, source_target_pairs={{0,128},{32,160},{64,192},{96,224},{128,0},{160,32},{192,64},{224,... | collective-permute-start | bytes 73736 | tf_op jit(solution)/shard_map/ppermute | solution.py:506
  89.4 6.0 %collective-permute-start.10 = (f32[48,128]{1,0:T(8,128)S(1)}, f32[48,128]{1,0:T(8,128)S(1)}, u32[]{:S(2)}, u32[]{:S(2)}) collective-permute-start(f32[48,128]{1,0:T(8,128)S(1)} %get-tuple-element.23), channel_id=1, source_target_pairs={{0,96},{32,128},{64,160},{96,192},{128,224},{160,0},{192,32},{224,... | collective-permute-start | bytes 73736 | tf_op jit(solution)/shard_map/ppermute | solution.py:506
  89.4 6.0 %collective-permute-start.9 = (f32[48,128]{1,0:T(8,128)S(1)}, f32[48,128]{1,0:T(8,128)S(1)}, u32[]{:S(2)}, u32[]{:S(2)}) collective-permute-start(f32[48,128]{1,0:T(8,128)S(1)} %get-tuple-element.24), channel_id=1, source_target_pairs={{0,64},{32,96},{64,128},{96,160},{128,192},{160,224},{192,0},{224,... | collective-permute-start | bytes 73736 | tf_op jit(solution)/shard_map/ppermute | solution.py:506
  92.7 4.4 %collective-permute-start.8 = (f32[48,128]{1,0:T(8,128)S(1)}, f32[48,128]{1,0:T(8,128)S(1)}, u32[]{:S(2)}, u32[]{:S(2)}) collective-permute-start(f32[48,128]{1,0:T(8,128)S(1)} %get-tuple-element.25), channel_id=1, source_target_pairs={{0,32},{32,64},{64,96},{96,128},{128,160},{160,192},{192,224},{224... | collective-permute-start | bytes 73736 | tf_op jit(solution)/shard_map/ppermute | solution.py:506
